TPU v7x, 256 devices: a whole 4x4x8 slice. The times are simulated.
256 devices in a mesh: leaf: 16 (over y, x), col: 16 (over z, core).
Axes of the slice: x: 4, y: 4, z: 8, core: 2. Of those that a mesh axis runs over, the one named last changes fastest.
Arguments:
- right_sides: bfloat16 [16, 2, 1792, 128], P('leaf', None, 'col'), may hold values from -6 to 6
- leaf_inverse: bfloat16 [16, 1792, 1792], P('leaf', 'col'), as said below
- upper_inverse: bfloat16 [16, 1792, 1792], P('leaf', 'col'), as said below
- leaf_update: bfloat16 [16, 4, 1792, 512], P('leaf', None, 'col'), may hold values from -0.0625 to 0.0625
- upper_update: bfloat16 [16, 4, 1792, 512], P('leaf', None, 'col'), may hold values from -0.0625 to 0.0625
- live_rows: int32 [16, 2], P('leaf'), may hold values from 896 to 1792, as said below
- tile_map: int32 [16, 2, 4, 512], P('leaf'), may hold values from 0 to 1791, as said below
Outputs:
- solution: bfloat16 [16, 2, 1792, 128], P('leaf', None, 'col')
Inputs may be any that keep to these rules, and one draw needn't show every extreme that they name: `leaf_inverse`: zero above the diagonal, nonzero on it. `upper_inverse`: zero above the diagonal, nonzero on it. `live_rows`: one supernode has all 1792 rows live and one has 896. `tile_map`: the rows of one tile are distinct and increasing.
All inputs are finite; a program needn't handle non-finite values.
Results may differ from a plain program's by a relative error of at most 0.0075.
Values may be sent and summed in bfloat16 or wider, within the bound.
No kernel may reach another device: no remote copies, remote signals or barrier semaphores. Data moves between devices by JAX's collectives and lax.ppermute only.
A program may use at most 64 MiB of HBM per device.

v0:
```python
import jax
import jax.numpy as jnp
from jax import lax
from jax.sharding import PartitionSpec as P


def forward_solve(inverse_rows, residual, row_mask, active):
    shares = (residual * row_mask).astype(jnp.bfloat16)
    empty = jnp.zeros((inverse_rows.shape[0], residual.shape[1]), jnp.float32)
    shard_rows = lax.all_gather(shares, "col", axis=0, tiled=True)
    solved = lax.cond(
        active,
        lambda: jnp.dot(inverse_rows, shard_rows, preferred_element_type=jnp.float32),
        lambda: empty,
    )
    return (solved * row_mask).astype(jnp.bfloat16)


def tile_terms(update_cols, solved, active):

    def tile_compute():
        return jnp.einsum("srt,rn->stn", update_cols, solved, preferred_element_type=jnp.float32)

    def tile_nothing():
        return jnp.zeros((update_cols.shape[0], update_cols.shape[2], solved.shape[1]), jnp.float32)

    local_terms = lax.cond(active, tile_compute, tile_nothing)
    return lax.psum(local_terms, "col")


def spread(summed, tile_rows, first_row, rows_dev):
    local_rows = tile_rows - first_row
    inside = (local_rows >= 0) & (local_rows < rows_dev)
    target = jnp.where(inside, local_rows, rows_dev)

    def one_slot(values, where_to):
        return (
            jnp.zeros((rows_dev, values.shape[1]), jnp.float32)
            .at[where_to]
            .add(values, mode="drop")
        )

    return jax.vmap(one_slot)(summed, target)


def pick_rows(fetched, tile_rows, first_row, rows_dev):
    local_rows = tile_rows - first_row
    inside = (local_rows >= 0) & (local_rows < rows_dev)
    chosen = fetched[jnp.clip(local_rows, 0, rows_dev - 1)]
    return jnp.where(inside[:, None], chosen, jnp.zeros_like(chosen))


def backward_solve(inverse_rows, solved, pulled, row_mask, active):
    scaled = ((solved.astype(jnp.float32) - pulled) * row_mask).astype(jnp.bfloat16)
    rhs_width = scaled.shape[1]
    row_count = inverse_rows.shape[0] * lax.axis_size("col")

    def rows_compute():
        return lax.dot_general(
            inverse_rows, scaled, (((0,), (0,)), ((), ())), preferred_element_type=jnp.float32
        )

    summed = lax.psum_scatter(
        lax.cond(active, rows_compute, lambda: jnp.zeros((row_count, rhs_width), jnp.float32)),
        "col",
        scatter_dimension=0,
        tiled=True,
    )
    return (summed * row_mask).astype(jnp.bfloat16)


def pull_terms(update_cols, tiles, active):

    def pull_compute():
        return jnp.einsum("srt,stn->rn", update_cols, tiles, preferred_element_type=jnp.float32)

    def pull_nothing():
        return jnp.zeros((update_cols.shape[1], tiles.shape[2]), jnp.float32)

    return lax.cond(active, pull_compute, pull_nothing)


def deliver(outgoing, height, leaf_id, leaf_count):
    owner = leaf_id // 2**height * 2**height + 2 ** (height - 1)
    onehot = (jnp.arange(leaf_count, dtype=jnp.int32) == owner).astype(jnp.float32)
    slot_table = onehot[:, None, None] * outgoing[None]
    return lax.psum_scatter(slot_table, "leaf", scatter_dimension=0, tiled=True)[0]


def fetch(answer_up, height, leaf_id):
    owner = leaf_id // 2**height * 2**height + 2 ** (height - 1)
    gathered = lax.all_gather(answer_up[None], "leaf", axis=0, tiled=True)
    return lax.dynamic_index_in_dim(gathered, owner, 0, keepdims=False)


def shards(
    right_sides, leaf_inverse, upper_inverse, leaf_update, upper_update, live_rows, tile_map
):
    leaf_count = lax.axis_size("leaf")
    depth = leaf_count.bit_length() - 1
    rows_dev = leaf_inverse.shape[1]
    rhs_width = right_sides.shape[3]
    tile_len = tile_map.shape[3]
    leaf_id = lax.axis_index("leaf")
    col_id = lax.axis_index("col")
    first_row = col_id * rows_dev
    row_ids = first_row + jnp.arange(rows_dev, dtype=jnp.int32)
    leaf_mask = (row_ids < live_rows[0, 0]).astype(jnp.float32)[:, None]
    upper_mask = (row_ids < live_rows[0, 1]).astype(jnp.float32)[:, None]
    node_level = jnp.zeros((), jnp.int32)
    for height in range(1, depth + 1):
        node_level = node_level + ((leaf_id % 2 ** (height - 1) == 0) & (leaf_id > 0)).astype(
            jnp.int32
        )
    always = jnp.array(True)
    solved_leaf = forward_solve(
        leaf_inverse[0], right_sides[0, 0].astype(jnp.float32), leaf_mask, always
    )
    summed = tile_terms(leaf_update[0, :depth], solved_leaf, always)
    pieces = spread(summed, tile_map[0, 0, :depth], first_row, rows_dev)
    outgoing = [None] + [pieces[height - 1] for height in range(1, depth + 1)]
    residual_up = right_sides[0, 1].astype(jnp.float32)
    solved_up = jnp.zeros((rows_dev, rhs_width), jnp.bfloat16)
    for height in range(1, depth + 1):
        residual_up = residual_up - deliver(outgoing[height], height, leaf_id, leaf_count)
        active = node_level == height
        solved = forward_solve(upper_inverse[0], residual_up, upper_mask, active)
        solved_up = jnp.where(active, solved, solved_up)
        slot_count = depth - height
        if slot_count > 0:
            summed = tile_terms(upper_update[0, :slot_count], solved, active)
            pieces = spread(summed, tile_map[0, 1, :slot_count], first_row, rows_dev)
            for slot_idx in range(slot_count):
                outgoing[height + 1 + slot_idx] = outgoing[height + 1 + slot_idx] + pieces[slot_idx]
    answer_up = jnp.zeros((rows_dev, rhs_width), jnp.bfloat16)
    tiles_leaf = [None] * depth
    tiles_upper = jnp.zeros((depth, tile_len, rhs_width), jnp.bfloat16)
    for height in range(depth, 0, -1):
        active = node_level == height
        slot_count = depth - height
        if slot_count > 0:
            pulled = pull_terms(upper_update[0, :slot_count], tiles_upper[:slot_count], active)
        else:
            pulled = jnp.zeros((rows_dev, rhs_width), jnp.float32)
        answer = backward_solve(upper_inverse[0], solved_up, pulled, upper_mask, active)
        answer_up = jnp.where(active, answer, answer_up)
        fetched = fetch(answer_up, height, leaf_id)
        slot_now = jnp.clip(height - node_level - 1, 0, depth - 1)
        valid = (node_level > 0) & (node_level < height)
        upper_map = lax.dynamic_index_in_dim(tile_map[0, 1], slot_now, 0, keepdims=False)
        leaf_part = pick_rows(fetched, tile_map[0, 0, height - 1], first_row, rows_dev)
        upper_part = pick_rows(fetched, upper_map, first_row, rows_dev)
        upper_part = jnp.where(valid, upper_part, jnp.zeros_like(upper_part))
        both = (
            lax.psum(jnp.stack([leaf_part, upper_part]), "col")
            .astype(jnp.float32)
            .astype(jnp.bfloat16)
        )
        tiles_leaf[height - 1] = both[0]
        updated = lax.dynamic_update_index_in_dim(tiles_upper, both[1], slot_now, 0)
        tiles_upper = jnp.where(valid, updated, tiles_upper)
    pulled = pull_terms(leaf_update[0, :depth], jnp.stack(tiles_leaf), always)
    answer_leaf = backward_solve(leaf_inverse[0], solved_leaf, pulled, leaf_mask, always)
    return jnp.stack([answer_leaf, answer_up])[None]


def solution(mesh):
    placed = (
        P("leaf", None, "col", None),
        P("leaf", "col", None),
        P("leaf", "col", None),
        P("leaf", None, "col", None),
        P("leaf", None, "col", None),
        P("leaf", None),
        P("leaf", None, None, None),
    )
    return jax.shard_map(
        shards, mesh=mesh, in_specs=placed, out_specs=P("leaf", None, "col", None), check_vma=False
    )
```

profile of v0, /device:TPU:4, one launch (start us, length us, event | category | flops | bytes accessed | tf_op | source)
XLA Modules:
  0.0 1756.1 jit_solution(690837087671866343)
XLA Ops:
  9.4 21.2 %all_gather.27 = bf16[1792,128]{1,0:T(8,128)(2,1)S(1)} all-gather(bf16[112,128]{1,0:T(8,128)(2,1)S(1)} %fusion.53), channel_id=1, replica_groups=mesh['leaf'=16,'col'=16] {'col'}, dimensions={0}, use_global_device_ids=true | all-gather | bytes 487424 | tf_op jit(solution)/shard_map/all_gather | solution.py:10
  34.5 108.2 %all-reduce.13.cloned.1.call-done = f32[4,512,128]{1,2,0:T(8,128)} async-done(((f32[4,512,128]{1,2,0:T(8,128)}), f32[4,512,128]{1,2,0:T(8,128)}) %all-reduce.13.cloned.1.call-update) | async-done | bytes 1048592 | tf_op jit(solution)/shard_map/psum | solution.py:28
  158.6 77.5 %reduce-scatter.38.cloned.1.call-done = f32[1,112,128]{2,1,0:T(8,128)} async-done(((f32[16,112,128]{2,1,0:T(8,128)}), f32[1,112,128]{2,1,0:T(8,128)}) %reduce-scatter.38.cloned.1.call-update) | async-done | bytes 57360
  257.0 109.0 %all-reduce.15.cloned.1.call-done = f32[3,512,128]{2,1,0:T(8,128)} async-done(((f32[3,512,128]{2,1,0:T(8,128)}), f32[3,512,128]{2,1,0:T(8,128)}) %all-reduce.15.cloned.1.call-update) | async-done | bytes 786448 | tf_op jit(solution)/shard_map/psum | solution.py:28
  377.1 78.3 %reduce-scatter.40.cloned.1.call-done = f32[1,112,128]{2,1,0:T(8,128)} async-done(((f32[16,112,128]{2,1,0:T(8,128)}), f32[1,112,128]{2,1,0:T(8,128)}) %reduce-scatter.40.cloned.1.call-update) | async-done | bytes 57360
  456.3 18.7 %all_gather.29 = bf16[1792,128]{1,0:T(8,128)(2,1)S(1)} all-gather(bf16[112,128]{1,0:T(8,128)(2,1)S(1)} %get-tuple-element.234), channel_id=1, replica_groups=mesh['leaf'=16,'col'=16] {'col'}, dimensions={0}, use_global_device_ids=true | all-gather | bytes 487424 | tf_op jit(solution)/shard_map/all_gather | solution.py:10
  476.6 107.9 %all-reduce.17.cloned.1.call-done = f32[2,512,128]{2,1,0:T(8,128)} async-done(((f32[2,512,128]{2,1,0:T(8,128)}), f32[2,512,128]{2,1,0:T(8,128)}) %all-reduce.17.cloned.1.call-update) | async-done | bytes 524304 | tf_op jit(solution)/shard_map/psum | solution.py:28
  592.1 79.1 %reduce-scatter.42.cloned.1.call-done = f32[1,112,128]{2,1,0:T(8,128)} async-done(((f32[16,112,128]{2,1,0:T(8,128)}), f32[1,112,128]{2,1,0:T(8,128)}) %reduce-scatter.42.cloned.1.call-update) | async-done | bytes 57360
  672.2 18.7 %all_gather.30 = bf16[1792,128]{1,0:T(8,128)(2,1)S(1)} all-gather(bf16[112,128]{1,0:T(8,128)(2,1)S(1)} %multiply_convert_fusion.7), channel_id=1, replica_groups=mesh['leaf'=16,'col'=16] {'col'}, dimensions={0}, use_global_device_ids=true | all-gather | bytes 487424 | tf_op jit(solution)/shard_map/all_gather | solution.py:10
  691.8 106.9 %all-reduce.19.cloned.1.call-done = f32[1,512,128]{2,1,0:T(8,128)} async-done(((f32[1,512,128]{2,1,0:T(8,128)}), f32[1,512,128]{2,1,0:T(8,128)}) %all-reduce.19.cloned.1.call-update) | async-done | bytes 262160 | tf_op jit(solution)/shard_map/psum | solution.py:28
  803.8 79.3 %reduce-scatter.44.cloned.1.call-done = f32[1,112,128]{2,1,0:T(8,128)} async-done(((f32[16,112,128]{2,1,0:T(8,128)}), f32[1,112,128]{2,1,0:T(8,128)}) %reduce-scatter.44.cloned.1.call-update) | async-done | bytes 57360
  906.3 52.8 %reduce-scatter.28.cloned.1.call-done = f32[112,128]{1,0:T(8,128)} async-done(((f32[1792,128]{1,0:T(8,128)}), f32[112,128]{1,0:T(8,128)}) %reduce-scatter.28.cloned.1.call-update) | async-done | bytes 57360 | tf_op jit(solution)/shard_map/reduce_scatter | solution.py:63
  960.0 23.5 %all-gather = bf16[1792,128]{1,0:T(8,128)(2,1)S(1)} all-gather(bf16[112,128]{1,0:T(8,128)(2,1)S(1)} %fusion.60), channel_id=2, replica_groups=mesh['leaf'=16,'col'=16] {'leaf'}, dimensions={0}, use_global_device_ids=true | all-gather | bytes 487424 | tf_op jit(solution)/shard_map/all_gather | solution.py:92
  987.3 107.1 %all-reduce.21.cloned.1.call-done = bf16[2,512,128]{2,1,0:T(8,128)(2,1)} async-done(((bf16[2,512,128]{2,1,0:T(8,128)(2,1)}), bf16[2,512,128]{2,1,0:T(8,128)(2,1)}) %all-reduce.21.cloned.1.call-update) | async-done | bytes 262160 | tf_op jit(solution)/shard_map/psum | solution.py:155
  1096.6 58.6 %reduce-scatter.30.cloned.1.call-done = f32[112,128]{1,0:T(8,128)} async-done(((f32[1792,128]{1,0:T(8,128)}), f32[112,128]{1,0:T(8,128)}) %reduce-scatter.30.cloned.1.call-update) | async-done | bytes 57360 | tf_op jit(solution)/shard_map/reduce_scatter | solution.py:63
  1156.2 23.6 %all-gather.1 = bf16[1792,128]{1,0:T(8,128)(2,1)S(1)} all-gather(bf16[112,128]{1,0:T(8,128)(2,1)S(1)} %fusion.61), channel_id=3, replica_groups=mesh['leaf'=16,'col'=16] {'leaf'}, dimensions={0}, use_global_device_ids=true | all-gather | bytes 487424 | tf_op jit(solution)/shard_map/all_gather | solution.py:92
  1183.6 107.0 %all-reduce.23.cloned.1.call-done = bf16[2,512,128]{2,1,0:T(8,128)(2,1)} async-done(((bf16[2,512,128]{2,1,0:T(8,128)(2,1)}), bf16[2,512,128]{2,1,0:T(8,128)(2,1)}) %all-reduce.23.cloned.1.call-update) | async-done | bytes 262160 | tf_op jit(solution)/shard_map/psum | solution.py:155
  1293.9 58.4 %reduce-scatter.32.cloned.1.call-done = f32[112,128]{1,0:T(8,128)} async-done(((f32[1792,128]{1,0:T(8,128)}), f32[112,128]{1,0:T(8,128)}) %reduce-scatter.32.cloned.1.call-update) | async-done | bytes 57360 | tf_op jit(solution)/shard_map/reduce_scatter | solution.py:63
  1353.2 23.6 %all-gather.2 = bf16[1792,128]{1,0:T(8,128)(2,1)S(1)} all-gather(bf16[112,128]{1,0:T(8,128)(2,1)S(1)} %fusion.62), channel_id=4, replica_groups=mesh['leaf'=16,'col'=16] {'leaf'}, dimensions={0}, use_global_device_ids=true | all-gather | bytes 487424 | tf_op jit(solution)/shard_map/all_gather | solution.py:92
  1381.7 107.2 %all-reduce.25.cloned.1.call-done = bf16[2,512,128]{2,1,0:T(8,128)(2,1)} async-done(((bf16[2,512,128]{2,1,0:T(8,128)(2,1)}), bf16[2,512,128]{2,1,0:T(8,128)(2,1)}) %all-reduce.25.cloned.1.call-update) | async-done | bytes 262160 | tf_op jit(solution)/shard_map/psum | solution.py:155
  1491.0 58.9 %reduce-scatter.34.cloned.1.call-done = f32[112,128]{1,0:T(8,128)} async-done(((f32[1792,128]{1,0:T(8,128)}), f32[112,128]{1,0:T(8,128)}) %reduce-scatter.34.cloned.1.call-update) | async-done | bytes 57360 | tf_op jit(solution)/shard_map/reduce_scatter | solution.py:63
  1550.7 23.6 %all-gather.3 = bf16[1792,128]{1,0:T(8,128)(2,1)S(1)} all-gather(bf16[112,128]{1,0:T(8,128)(2,1)S(1)} %fusion.63), channel_id=5, replica_groups=mesh['leaf'=16,'col'=16] {'leaf'}, dimensions={0}, use_global_device_ids=true | all-gather | bytes 487424 | tf_op jit(solution)/shard_map/all_gather | solution.py:92
  1580.2 106.3 %all-reduce.27.cloned.1.call-done = bf16[2,512,128]{2,1,0:T(8,128)(2,1)} async-done(((bf16[2,512,128]{2,1,0:T(8,128)(2,1)}), bf16[2,512,128]{2,1,0:T(8,128)(2,1)}) %all-reduce.27.cloned.1.call-update) | async-done | bytes 262160 | tf_op jit(solution)/shard_map/psum | solution.py:155
  1689.3 58.7 %reduce-scatter.36.cloned.1.call-done = f32[112,128]{1,0:T(8,128)} async-done(((f32[1792,128]{1,0:T(8,128)}), f32[112,128]{1,0:T(8,128)}) %reduce-scatter.36.cloned.1.call-update) | async-done | bytes 57360 | tf_op jit(solution)/shard_map/reduce_scatter | solution.py:63
  (241 shorter events, 128.8 us)
Async XLA Ops:
  6.5 136.2 %all-reduce.13.cloned.1.call-start = ((), (), s32[]{:S(2)}) async-start(), calls=%async_computation.9 | async-start | bytes 2097152 | tf_op jit(solution)/shard_map/psum | solution.py:28
  32.3 203.8 %reduce-scatter.38.cloned.1.call-start = ((), (), s32[]{:S(2)}) async-start(), calls=%async_computation.22 | async-start | bytes 974848
  156.9 209.0 %all-reduce.15.cloned.1.call-start = ((), (), s32[]{:S(2)}) async-start(), calls=%async_computation.10 | async-start | bytes 1572864 | tf_op jit(solution)/shard_map/psum | solution.py:28
  158.5 77.6 %copy-start.24 = (bf16[1,2,112,128]{3,2,1,0:T(8,128)(2,1)S(1)}, bf16[1,2,112,128]{3,2,1,0:T(8,128)(2,1)}, u32[]{:S(2)}) copy-start(bf16[1,2,112,128]{3,2,1,0:T(8,128)(2,1)} %param.35) | copy-start | bytes 172036
  158.6 97.1 %copy-start.1 = (bf16[1,112,1792]{2,1,0:T(8,128)(2,1)S(1)}, bf16[1,112,1792]{2,1,0:T(8,128)(2,1)}, u32[]{:S(2)}) copy-start(bf16[1,112,1792]{2,1,0:T(8,128)(2,1)} %param.37) | copy-start | bytes 1204228
  256.8 198.6 %reduce-scatter.40.cloned.1.call-start = ((), (), s32[]{:S(2)}) async-start(), calls=%async_computation.23 | async-start | bytes 974848
  376.2 208.2 %all-reduce.17.cloned.1.call-start = ((), (), s32[]{:S(2)}) async-start(), calls=%async_computation.11 | async-start | bytes 1048576 | tf_op jit(solution)/shard_map/psum | solution.py:28
  377.1 78.4 %copy-start.20 = (f32[1,112,128]{2,1,0:T(8,128)S(1)}, f32[1,112,128]{2,1,0:T(8,128)}, u32[]{:S(2)}) copy-start(f32[1,112,128]{2,1,0:T(8,128)} %reduce-scatter.38.cloned.1.call-done) | copy-start | bytes 172036
  476.5 194.8 %reduce-scatter.42.cloned.1.call-start = ((), (), s32[]{:S(2)}) async-start(), calls=%async_computation.24 | async-start | bytes 974848
  592.0 206.7 %all-reduce.19.cloned.1.call-start = ((), (), s32[]{:S(2)}) async-start(), calls=%async_computation.12 | async-start | bytes 524288 | tf_op jit(solution)/shard_map/psum | solution.py:28
  691.7 191.4 %reduce-scatter.44.cloned.1.call-start = ((), (), s32[]{:S(2)}) async-start(), calls=%async_computation.25 | async-start | bytes 974848
  803.7 79.4 %copy-start.22 = (f32[1,112,128]{2,1,0:T(8,128)S(1)}, f32[1,112,128]{2,1,0:T(8,128)}, u32[]{:S(2)}) copy-start(f32[1,112,128]{2,1,0:T(8,128)} %reduce-scatter.42.cloned.1.call-done) | copy-start | bytes 172036
  803.7 155.4 %reduce-scatter.28.cloned.1.call-start = ((), (), s32[]{:S(2)}) async-start(), calls=%async_computation.17 | async-start | bytes 974848 | tf_op jit(solution)/shard_map/reduce_scatter | solution.py:63
  902.8 192.6 %copy-start.11 = (bf16[112,128]{1,0:T(8,128)(2,1)}, bf16[112,128]{1,0:T(8,128)(2,1)S(1)}, u32[]{:S(2)}) copy-start(bf16[112,128]{1,0:T(8,128)(2,1)S(1)} %get-tuple-element.233) | copy-start | bytes 86020
  903.8 190.5 %all-reduce.21.cloned.1.call-start = ((), (), s32[]{:S(2)}) async-start(), calls=%async_computation.13 | async-start | bytes 524288 | tf_op jit(solution)/shard_map/psum | solution.py:155
  987.2 168.0 %reduce-scatter.30.cloned.1.call-start = ((), (), s32[]{:S(2)}) async-start(), calls=%async_computation.18 | async-start | bytes 974848 | tf_op jit(solution)/shard_map/reduce_scatter | solution.py:63
  1095.6 59.7 %copy-start.21 = (f32[112,128]{1,0:T(8,128)S(1)}, f32[112,128]{1,0:T(8,128)}, u32[]{:S(2)}) copy-start(f32[112,128]{1,0:T(8,128)} %reduce-scatter.28.cloned.1.call-done) | copy-start | bytes 172036
  1096.5 194.1 %all-reduce.23.cloned.1.call-start = ((), (), s32[]{:S(2)}) async-start(), calls=%async_computation.14 | async-start | bytes 524288 | tf_op jit(solution)/shard_map/psum | solution.py:155
  1183.5 168.7 %reduce-scatter.32.cloned.1.call-start = ((), (), s32[]{:S(2)}) async-start(), calls=%async_computation.19 | async-start | bytes 974848 | tf_op jit(solution)/shard_map/reduce_scatter | solution.py:63
  1293.8 195.2 %all-reduce.25.cloned.1.call-start = ((), (), s32[]{:S(2)}) async-start(), calls=%async_computation.15 | async-start | bytes 524288 | tf_op jit(solution)/shard_map/psum | solution.py:155
  1381.7 168.1 %reduce-scatter.34.cloned.1.call-start = ((), (), s32[]{:S(2)}) async-start(), calls=%async_computation.20 | async-start | bytes 974848 | tf_op jit(solution)/shard_map/reduce_scatter | solution.py:63
  1490.9 195.7 %all-reduce.27.cloned.1.call-start = ((), (), s32[]{:S(2)}) async-start(), calls=%async_computation.16 | async-start | bytes 524288 | tf_op jit(solution)/shard_map/psum | solution.py:155
  1579.3 168.7 %reduce-scatter.36.cloned.1.call-start = ((), (), s32[]{:S(2)}) async-start(), calls=%async_computation.21 | async-start | bytes 974848 | tf_op jit(solution)/shard_map/reduce_scatter | solution.py:63
  1580.2 106.3 %copy-start.17 = (bf16[128,112]{0,1:T(8,128)(2,1)S(1)}, bf16[128,112]{0,1:T(8,128)(2,1)}, u32[]{:S(2)}) copy-start(bf16[128,112]{0,1:T(8,128)(2,1)} %copy-done.16) | copy-start | bytes 86020
  (29 other events, 152.0 us)
Sparse Core Ops, SparseCore 0:
  32.4 110.2 all-reduce.12
  157.1 78.9 reduce-scatter.37
  256.9 108.9 all-reduce.14
  376.3 79.0 reduce-scatter.39
  476.6 107.7 all-reduce.16
  592.1 79.0 reduce-scatter.41
  691.8 106.8 all-reduce.18
  803.8 79.1 reduce-scatter.43
  903.9 55.1 reduce-scatter.27
  987.3 106.9 all-reduce.20
  1096.9 58.3 reduce-scatter.29
  1183.6 106.9 all-reduce.22
  1293.9 58.3 reduce-scatter.31
  1381.8 107.1 all-reduce.24
  1491.3 58.4 reduce-scatter.33
  1579.4 107.0 all-reduce.26
  1689.4 58.5 reduce-scatter.35
where the time goes:
time: 1760 us
  waiting for transfers between devices  1460 us (83%)
  blocking collectives  190 us (11%)
  other arithmetic  54.8 us (3%)
  local copies, waits for them, and re-layouts  31.1 us (2%)
    psum x4, waiting for transfers between devices, tile_terms(): return lax.psum(local_terms, 'col')  432 us
    psum x4, waiting for transfers between devices, shards(): lax.psum(jnp.stack([leaf_part, upper_part]), 'col').astype(jnp.float32)  428 us
    unnamed x21, waiting for transfers between devices  315 us
    reduce_scatter x5, waiting for transfers between devices, backward_solve(): lax.psum_scatter(lax.cond(active, rows_compute, lambda: jnp.zeros((row_co...  287 us
    all_gather x5, blocking collectives, forward_solve(): shard_rows = lax.all_gather(shares, 'col', axis=0, tiled=True)  96 us
    all_gather x4, blocking collectives, fetch(): gathered = lax.all_gather(answer_up[None], 'leaf', axis=0, tiled=True)  94.3 us
  transfers between devices with their start and end apart: 17, of which 17 were waited for; matrix products, arithmetic and copies ran while one was open for 0% of the time, Pallas kernels for 0%

commit v1 on v0

v1 whole, which is shorter than its diff:
```python
import jax
import jax.numpy as jnp
from jax import lax
from jax.sharding import PartitionSpec as P

BF = jnp.bfloat16
F32 = jnp.float32


def dot(a, b, ca, cb):
    return lax.dot_general(a, b, (((ca,), (cb,)), ((), ())), preferred_element_type=F32)


def split_dot(a, b, ca, cb):
    hi = a.astype(BF)
    lo = (a - hi.astype(F32)).astype(BF)
    n = a.shape[0]
    both = dot(jnp.concatenate([hi, lo], axis=0), b, ca, cb)
    return both[:n] + both[n:]


def shards(
    right_sides, leaf_inverse, upper_inverse, leaf_update, upper_update, live_rows, tile_map
):
    leaf_count = lax.axis_size("leaf")
    col_count = lax.axis_size("col")
    depth = leaf_count.bit_length() - 1
    rows_dev = leaf_inverse.shape[1]
    rows = leaf_inverse.shape[2]
    width = right_sides.shape[3]
    part = width // col_count
    tile_len = tile_map.shape[3]
    leaf_id = lax.axis_index("leaf")
    col_id = lax.axis_index("col")

    all_rows = lax.broadcasted_iota(jnp.int32, (1, rows), 1)
    mask_up = (all_rows < live_rows[0, 1]).astype(F32)
    rows_full = lax.broadcasted_iota(jnp.int32, (rows, 1), 0)
    own_rows = col_id * rows_dev + lax.broadcasted_iota(jnp.int32, (rows_dev, 1), 0)
    mask_leaf = (own_rows < live_rows[0, 0]).astype(F32)

    node_level = jnp.zeros((), jnp.int32)
    for height in range(1, depth + 1):
        node_level = node_level + ((leaf_id % 2 ** (height - 1) == 0) & (leaf_id > 0)).astype(
            jnp.int32
        )

    inv_up = lax.all_gather(upper_inverse[0], "col", axis=0, tiled=True)
    upd_up = lax.all_gather(upper_update[0, : depth - 1], "col", axis=1, tiled=True)

    picks = (
        tile_map[0][:, :, :, None] == lax.broadcasted_iota(jnp.int32, (1, 1, 1, rows), 3)
    ).astype(BF)
    pick_leaf, pick_up = picks[0], picks[1]

    both = lax.all_gather(right_sides[0], "col", axis=1, tiled=True)
    r_leaf = jnp.where(rows_full < live_rows[0, 0], both[0], jnp.zeros_like(both[0]))
    base_up = lax.dynamic_slice_in_dim(both[1].T, col_id * part, part, 0).astype(F32)

    y_leaf = (dot(leaf_inverse[0], r_leaf, 1, 0) * mask_leaf).astype(BF)
    terms = jnp.concatenate(
        [dot(y_leaf, leaf_update[0, s], 0, 0) for s in range(depth)], axis=1
    ).astype(BF)
    swapped = lax.all_to_all(
        terms.reshape(col_count, part, depth * tile_len), "col", 0, 0, tiled=False
    )
    z_leaf = jnp.sum(swapped.astype(F32), axis=0)
    acc = jnp.stack(
        [
            split_dot(z_leaf[:, s * tile_len : (s + 1) * tile_len], pick_leaf[s], 1, 0)
            for s in range(depth)
        ]
    )

    nodes = range(1, leaf_count)

    def level_of(node):
        return (node & -node).bit_length()

    y_up = jnp.zeros((part, rows), BF)
    for height in range(1, depth + 1):
        if height == 1:
            got = lax.ppermute(acc, "leaf", [(i, i + 1) for i in range(0, leaf_count, 2)])
            acc = jnp.where(leaf_id % 2 == 1, acc + got, 0.0)
        else:
            step = 2 ** (height - 2)
            ups = [i for i in nodes if level_of(i) == height]
            acc = lax.ppermute(acc, "leaf", [(i - step, i) for i in ups]) + lax.ppermute(
                acc, "leaf", [(i + step, i) for i in ups]
            )
        r = ((base_up - acc[0]) * mask_up).astype(BF)
        y = (dot(r, inv_up, 1, 1) * mask_up).astype(BF)
        y_up = jnp.where(node_level == height, y, y_up)
        acc = acc[1:]
        if height < depth:
            acc = acc + jnp.stack(
                [
                    split_dot(dot(y, upd_up[s], 1, 0), pick_up[s], 1, 0)
                    for s in range(depth - height)
                ]
            )

    x_up = jnp.zeros((part, rows), BF)
    above = None
    for height in range(depth, 0, -1):
        if height == depth:
            pulled = jnp.zeros((part, rows), F32)
        else:
            pulled = sum(
                dot(dot(above[s], pick_up[s], 1, 1).astype(BF), upd_up[s], 1, 1)
                for s in range(depth - height)
            )
        v = ((y_up.astype(F32) - pulled) * mask_up).astype(BF)
        x = (dot(v, inv_up, 1, 0) * mask_up).astype(BF)
        x_up = jnp.where(node_level == height, x, x_up)
        above = x[None] if above is None else jnp.concatenate([x[None], above])
        if height == 1:
            got = lax.ppermute(above, "leaf", [(i + 1, i) for i in range(0, leaf_count, 2)])
            above = jnp.where(leaf_id % 2 == 1, above, got)
        else:
            step = 2 ** (height - 2)
            ups = [i for i in nodes if level_of(i) == height]
            above = lax.ppermute(above, "leaf", [(i, i - step) for i in ups]) + lax.ppermute(
                above, "leaf", [(i, i + step) for i in ups]
            )

    tiles = jnp.concatenate(
        [dot(above[s], pick_leaf[s], 1, 1).astype(BF) for s in range(depth)], axis=1
    )
    tiles = lax.all_gather(tiles, "col", axis=0, tiled=True)
    pulled = sum(
        dot(leaf_update[0, s], tiles[:, s * tile_len : (s + 1) * tile_len], 1, 1)
        for s in range(depth)
    )
    v = ((y_leaf.astype(F32) - pulled) * mask_leaf).astype(BF)
    terms = dot(leaf_inverse[0], v, 0, 0).astype(BF).reshape(col_count, rows_dev, width)
    swapped = lax.all_to_all(terms, "col", 0, 0, tiled=False)
    x_leaf = (jnp.sum(swapped.astype(F32), axis=0) * mask_leaf).astype(BF)

    x_up = jnp.where(leaf_id > 0, x_up, jnp.zeros_like(x_up))
    up_rows = lax.all_to_all(
        x_up.reshape(part, col_count, rows_dev).transpose(1, 0, 2), "col", 0, 0, tiled=False
    )
    up_rows = up_rows.reshape(width, rows_dev).T
    return jnp.stack([x_leaf, up_rows])[None]


def solution(mesh):
    placed = (
        P("leaf", None, "col", None),
        P("leaf", "col", None),
        P("leaf", "col", None),
        P("leaf", None, "col", None),
        P("leaf", None, "col", None),
        P("leaf", None),
        P("leaf", None, None, None),
    )
    return jax.shard_map(
        shards, mesh=mesh, in_specs=placed, out_specs=P("leaf", None, "col", None), check_vma=False
    )
```

time: 1760 us -> 275 us (0.16)
  waiting for transfers between devices: 1460 us -> 82.6 us
  blocking collectives: 190 us -> 43.8 us
  matrix products: 3.18 us -> 75.2 us
  other arithmetic: 54.8 us -> 12.3 us
  starting transfers between devices: 0.67 us -> 30.2 us
  local copies, waits for them, and re-layouts: 31.1 us -> 11.9 us
    psum x8 -> x0, waiting for transfers between devices: 860 us -> none  [the longest x4 432 us: tile_terms(): return lax.psum(local_terms, 'col')]
    unnamed x21 -> x2, waiting for transfers between devices: 315 us -> 0.72 us
    reduce_scatter x5 -> x0, waiting for transfers between devices: 287 us -> none  [backward_solve(): lax.psum_scatter(lax.cond(active, rows_compute, lambda: jnp.zeros((row_co...]
    all_gather x9 -> x2, blocking collectives: 190 us -> 43.8 us  [the longest x1 25.1 us: shards(): both = lax.all_gather(right_sides[0], 'col', axis=1, tiled=True)]
    dot_general x7 -> x43, matrix products: 3.18 us -> 75.2 us  [dot(): lax.dot_general(a, b, (((ca,), (cb,)), ((), ())), preferred_element_type=...]
    all_to_all x0 -> x3, waiting for transfers between devices: none -> 28.6 us  [the longest x1 14.7 us: shards(): swapped = lax.all_to_all(terms, 'col', 0, 0, tiled=False)]
    ppermute x0 -> x14, waiting for transfers between devices: none -> 28.5 us  [the longest x3 16 us: shards(): lax.ppermute(above, 'leaf', [(i, i - step) for i in ups])]
    unnamed x12 -> x1, other arithmetic: 27.6 us -> 0.01 us
  transfers between devices with their start and end apart: 17 -> 19, of which waited for: 17 -> 10; matrix products, arithmetic and copies ran while one was open for 0% -> 16% of each run, Pallas kernels for 0% -> 0%
where the time goes in v1:
time: 275 us; the launch traced here: 270 us
  waiting for transfers between devices  82.6 us (30%)
  matrix products  75.2 us (27%)
  blocking collectives  43.8 us (16%)
  starting transfers between devices  30.2 us (11%)
  between operations  14.1 us (5%)
  other arithmetic  12.3 us (4%)
  local copies, waits for them, and re-layouts  11.9 us (4%)
    dot_general x43, matrix products, dot(): lax.dot_general(a, b, (((ca,), (cb,)), ((), ())), preferred_element_type=...  75.2 us
    all_gather x1, blocking collectives, shards(): both = lax.all_gather(right_sides[0], 'col', axis=1, tiled=True)  25.1 us
    all_gather x1, waiting for transfers between devices, shards(): lax.all_gather(upper_update[0, :depth - 1], 'col', axis=1, tiled=True)  24.8 us
    all_gather x1, blocking collectives, shards(): tiles = lax.all_gather(tiles, 'col', axis=0, tiled=True)  18.7 us
    ppermute x3, waiting for transfers between devices, shards(): lax.ppermute(above, 'leaf', [(i, i - step) for i in ups])  16 us
    all_to_all x1, waiting for transfers between devices, shards(): swapped = lax.all_to_all(terms, 'col', 0, 0, tiled=False)  14.7 us
    all_to_all x1, waiting for transfers between devices, shards(): lax.all_to_all(terms.reshape(col_count, part, depth * tile_len), 'col', 0...  13.9 us
    ppermute x3, waiting for transfers between devices, shards(): lax.ppermute(acc, 'leaf', [(i - step, i) for i in ups])  7.3 us
  transfers between devices with their start and end apart: 19, of which 10 were waited for; matrix products, arithmetic and copies ran while one was open for 16% of the time, Pallas kernels for 0%

profile of v1, /device:TPU:4, one launch (start us, length us, event | category | flops | bytes accessed | tf_op | source)
XLA Modules:
  0.0 270.1 jit_solution(10136190612062378976)
XLA Ops:
  12.5 25.1 %all-gather = bf16[1,2,1792,128]{3,1,0,2:T(2,128)(2,1)S(1)} all-gather(bf16[1,2,112,128]{3,1,0,2:T(2,128)(2,1)S(1)} %copy.25), channel_id=2, replica_groups=mesh['leaf'=16,'col'=16] {'col'}, dimensions={2}, use_global_device_ids=true | all-gather | bytes 974848 | tf_op jit(solution)/shard_map/all_gather | solution.py:56
  41.8 3.8 %all-to-all-start = ((bf16[16,8,2048]{2,1,0:T(8,128)(2,1)}), bf16[16,8,2048]{2,1,0:T(8,128)(2,1)S(1)}, u32[]{:S(2)}, u32[]{:S(2)}) async-start(bf16[16,8,2048]{2,1,0:T(8,128)(2,1)} %pad_maximum_fusion), calls=%async_computation | async-start | bytes 1048576 | tf_op jit(solution)/shard_map/all_to_all | solution.py:64
  45.6 6.7 %iota_compare_fusion = pred[2,4,512,1792]{3,2,1,0:T(32,128)(4,1)} fusion(s32[2,4,512]{2,1,0:T(4,128)S(1)} %bitcast.352), kind=kLoop, calls=%fused_computation | loop fusion | flops 7340032 | bytes 7356416 | tf_op jit(solution)/shard_map/eq | solution.py:52
  53.9 13.9 %all-to-all-done = bf16[16,8,2048]{2,1,0:T(8,128)(2,1)S(1)} async-done(((bf16[16,8,2048]{2,1,0:T(8,128)(2,1)}), bf16[16,8,2048]{2,1,0:T(8,128)(2,1)S(1)}, u32[]{:S(2)}, u32[]{:S(2)}) %all-to-all-start) | async-done | bytes 524320 | tf_op jit(solution)/shard_map/all_to_all | solution.py:64
  76.0 3.8 %collective-permute-start = (f32[4,8,1792]{2,1,0:T(8,128)}, f32[4,8,1792]{2,1,0:T(8,128)}, u32[]{:S(2)}, u32[]{:S(2)}) collective-permute-start(f32[4,8,1792]{2,1,0:T(8,128)} %pad_maximum_fusion.1), channel_id=1, source_target_pairs={{0,16},{32,48},{64,80},{96,112},{128,144},{160,176},{192,208},{224... | collective-permute-start | bytes 688136 | tf_op jit(solution)/shard_map/ppermute | solution.py:83
  82.3 2.6 collective-permute-done
  86.6 5.2 %fusion.77 = bf16[8,1792]{1,0:T(8,128)(2,1)} fusion(bf16[1,1792,1792]{2,1,0:T(8,128)(2,1)} %all-gather.6.cloned.1.call-done, f32[4,8,1792]{2,1,0:T(8,128)S(1)} %add_select_fusion, bf16[1,1,1792,8]{2,3,1,0:T(8,128)(2,1)S(1)} %copy.34, f32[1792]{0:T(1024)S(1)} %fusion.216), kind=kOutput, calls=%fused_computation.60 | convolution fusion | flops 51466240 | bytes 6553600 | tf_op jit(solution)/shard_map/dot_general | solution.py:11
  91.8 24.8 %all-gather.8.cloned.1.call-done = bf16[1,3,1792,512]{3,2,1,0:T(8,128)(2,1)} async-done(((bf16[1,3,112,512]{3,2,1,0:T(8,128)(2,1)}), bf16[1,3,1792,512]{3,2,1,0:T(8,128)(2,1)}) %all-gather.8.cloned.1.call-update) | async-done | bytes 5505040 | tf_op jit(solution)/shard_map/all_gather | solution.py:49
  128.6 5.8 %collective-permute-done.1 = f32[3,8,1792]{2,1,0:T(8,128)S(1)} collective-permute-done((f32[3,8,1792]{2,1,0:T(8,128)S(1)}, f32[3,8,1792]{2,1,0:T(8,128)S(1)}, u32[]{:S(2)}, u32[]{:S(2)}) %collective-permute-start.1) | collective-permute-done | bytes 172064 | tf_op jit(solution)/shard_map/ppermute | solution.py:88
  148.5 4.6 %fusion.86 = f32[8,1792]{1,0:T(8,128)S(1)} fusion(bf16[1,1792,1792]{2,1,0:T(8,128)(2,1)} %all-gather.6.cloned.1.call-done, f32[1,8,1792]{2,1,0:T(8,128)S(1)} %collective-permute-done.5, f32[1,8,1792]{2,1,0:T(8,128)S(1)} %collective-permute-done.6, bf16[1,1,1792,8]{2,3,1,0:T(8,128)(2,1)} %copy-done.6, bf16[8,1792]{1,0:T(8,128)(2,1)} %copy-done.9, ...), kind=kOutput, calls=%fused_computation.65 | convolution fusion | flops 51552256 | bytes 6716420 | tf_op jit(solution)/shard_map/dot_general | solution.py:11
  153.1 3.8 %fusion.65 = bf16[8,1792]{1,0:T(8,128)(2,1)S(1)} fusion(bf16[1,1792,1792]{2,1,0:T(8,128)(2,1)} %all-gather.6.cloned.1.call-done, f32[8,1792]{1,0:T(8,128)S(1)} %fusion.86, f32[1792]{0:T(1024)S(1)} %fusion.216), kind=kOutput, calls=%fused_computation.56 | convolution fusion | flops 51437568 | bytes 6515712 | tf_op jit(solution)/shard_map/dot_general | solution.py:11
  158.9 4.9 %fusion.62 = bf16[8,1792]{1,0:T(8,128)(2,1)S(1)} fusion(bf16[1,1792,1792]{2,1,0:T(8,128)(2,1)} %all-gather.6.cloned.1.call-done, f32[8,1792]{1,0:T(8,128)S(1)} %fusion.86, bf16[8,512]{1,0:T(8,128)(2,1)S(1)} %convolution_convert_fusion.9, bf16[1,3,1792,512]{3,2,1,0:T(8,128)(2,1)} %all-gather.8.cloned.1.call-done, f32[1792]{0:T(1024)S(1)} %fusion.216), kind=kOutput, calls=%fused_computation.55 | convolution fusion | flops 66131968 | bytes 8368128 | tf_op jit(solution)/shard_map/dot_general | solution.py:11
  165.8 15.2 %collective-permute-done.9 = bf16[2,8,1792]{2,1,0:T(8,128)(2,1)S(1)} collective-permute-done((bf16[2,8,1792]{2,1,0:T(8,128)(2,1)S(1)}, bf16[2,8,1792]{2,1,0:T(8,128)(2,1)S(1)}, u32[]{:S(2)}, u32[]{:S(2)}) %collective-permute-start.9) | collective-permute-done | bytes 57376 | tf_op jit(solution)/shard_map/ppermute | solution.py:123
  181.0 2.7 fusion.101
  183.7 3.1 %fusion.81 = bf16[8,1792]{1,0:T(8,128)(2,1)S(1)} fusion(f32[8,1792]{1,0:T(8,128)S(1)} %fusion.86, f32[8,1792]{1,0:T(8,128)S(1)} %fusion.101, bf16[1,3,1792,512]{3,2,1,0:T(8,128)(2,1)} %all-gather.8.cloned.1.call-done, pred[2,4,512,1792]{3,2,1,0:T(32,128)(4,1)} %iota_compare_fusion, bf16[2,8,1792]{2,1,0:T(8,128)(2,1)S(1)} %add.144, f32[1792]{0:T(1024)S(1)} %fusion.216), kind=kOutput, calls=%fused_computation.62 | convolution fusion | flops 29421568 | bytes 2932736 | tf_op jit(solution)/shard_map/dot_general | solution.py:11
  186.8 3.8 %fusion.59 = bf16[8,1792]{1,0:T(8,128)(2,1)S(1)} fusion(bf16[8,1792]{1,0:T(8,128)(2,1)S(1)} %fusion.81, bf16[1,1792,1792]{2,1,0:T(8,128)(2,1)} %all-gather.6.cloned.1.call-done, f32[1792]{0:T(1024)S(1)} %fusion.216), kind=kOutput, calls=%fused_computation.54 | convolution fusion | flops 51408896 | bytes 6487040 | tf_op jit(solution)/shard_map/dot_general | solution.py:11
  195.3 2.7 fusion.102
  198.0 3.1 %convolution_add_fusion.1 = f32[8,1792]{1,0:T(8,128)S(1)} fusion(f32[8,1792]{1,0:T(8,128)S(1)} %fusion.102, bf16[1,3,1792,512]{3,2,1,0:T(8,128)(2,1)} %all-gather.8.cloned.1.call-done, pred[2,4,512,1792]{3,2,1,0:T(32,128)(4,1)} %iota_compare_fusion, bf16[3,8,1792]{2,1,0:T(8,128)(2,1)S(1)} %add.146), kind=kOutput, calls=%fused_computation.39 | convolution fusion | flops 29378560 | bytes 2895872 | tf_op jit(solution)/shard_map/dot_general | solution.py:11
  201.1 3.1 %fusion.82 = bf16[8,1792]{1,0:T(8,128)(2,1)S(1)} fusion(f32[8,1792]{1,0:T(8,128)S(1)} %fusion.86, f32[8,1792]{1,0:T(8,128)S(1)} %convolution_add_fusion.1, bf16[1,3,1792,512]{3,2,1,0:T(8,128)(2,1)} %all-gather.8.cloned.1.call-done, pred[2,4,512,1792]{3,2,1,0:T(32,128)(4,1)} %iota_compare_fusion, bf16[3,8,1792]{2,1,0:T(8,128)(2,1)S(1)} %add.146, ...), kind=kOutput, calls=%fused_computation.63 | convolution fusion | flops 29421568 | bytes 2932736 | tf_op jit(solution)/shard_map/dot_general | solution.py:11
  204.2 3.8 %select_select_fusion = (bf16[8,1792]{1,0:T(8,128)(2,1)S(1)}, bf16[8,1792]{1,0:T(8,128)(2,1)S(1)}) fusion(bf16[8,1792]{1,0:T(8,128)(2,1)S(1)} %fusion.59, bf16[8,1792]{1,0:T(8,128)(2,1)S(1)} %fusion.62, bf16[8,1792]{1,0:T(8,128)(2,1)S(1)} %fusion.65, pred[]{:T(512)S(6)} %gt.2, pred[]{:T(512)S(6)} %eq.63, pred[]{:T(512)S(6)} %eq.62, pred[]{:T(512)S(6)} %eq.61, ...), kind=kOutput, calls=%fused_computation.202 | convolution fusion | flops 51480576 | bytes 6601733 | tf_op jit(solution)/shard_map/dot_general | solution.py:11
  210.2 4.6 %all-to-all-start.2 = ((bf16[16,8,112]{2,1,0:T(8,128)(2,1)}), bf16[16,8,112]{2,1,0:T(8,128)(2,1)S(1)}, u32[]{:S(2)}, u32[]{:S(2)}) async-start(bf16[16,8,112]{2,1,0:T(8,128)(2,1)} %bitcast.341), calls=%async_computation.2 | async-start | bytes 65536 | tf_op jit(solution)/shard_map/all_to_all | solution.py:141
  222.4 18.7 %all_gather.15 = bf16[128,2048]{1,0:T(8,128)(2,1)S(1)} all-gather(bf16[8,2048]{1,0:T(8,128)(2,1)S(1)} %pad_maximum_fusion.5), channel_id=1, replica_groups=mesh['leaf'=16,'col'=16] {'col'}, dimensions={0}, use_global_device_ids=true | all-gather | bytes 557056 | tf_op jit(solution)/shard_map/all_gather | solution.py:130
  243.1 4.6 %all-to-all-start.1 = ((bf16[16,112,128]{2,1,0:T(8,128)(2,1)}), bf16[16,112,128]{2,1,0:T(8,128)(2,1)S(1)}, u32[]{:S(2)}, u32[]{:S(2)}) async-start(bf16[16,112,128]{2,1,0:T(8,128)(2,1)} %bitcast.58), calls=%async_computation.1 | async-start | bytes 917504 | tf_op jit(solution)/shard_map/all_to_all | solution.py:137
  247.9 14.7 %all-to-all-done.1 = bf16[16,112,128]{2,1,0:T(8,128)(2,1)S(1)} async-done(((bf16[16,112,128]{2,1,0:T(8,128)(2,1)}), bf16[16,112,128]{2,1,0:T(8,128)(2,1)S(1)}, u32[]{:S(2)}, u32[]{:S(2)}) %all-to-all-start.1) | async-done | bytes 458784 | tf_op jit(solution)/shard_map/all_to_all | solution.py:137
  (140 shorter events, 71.0 us)
Async XLA Ops:
  6.5 33.7 %copy-start.2 = (bf16[1,4,112,512]{3,2,1,0:T(8,128)(2,1)S(1)}, bf16[1,4,112,512]{3,2,1,0:T(8,128)(2,1)}, u32[]{:S(2)}) copy-start(bf16[1,4,112,512]{3,2,1,0:T(8,128)(2,1)} %param.10) | copy-start | bytes 1376260
  6.5 39.1 %copy-start.12 = (s32[1,2,4,512]{3,2,1,0:T(4,128)S(1)}, s32[1,2,4,512]{3,2,1,0:T(4,128)}, u32[]{:S(2)}) copy-start(s32[1,2,4,512]{3,2,1,0:T(4,128)} %param.13) | copy-start | bytes 49156
  6.5 79.4 %all-gather.6.cloned.1.call-start = ((), (), s32[]{:S(2)}) async-start(), calls=%async_computation.3 | async-start | bytes 6823936 | tf_op jit(solution)/shard_map/all_gather | solution.py:48
  7.3 109.4 %all-gather.8.cloned.1.call-start = ((), (), s32[]{:S(2)}) async-start(), calls=%async_computation.4 | async-start | bytes 5849088 | tf_op jit(solution)/shard_map/all_gather | solution.py:49
  11.9 40.5 %copy-start.13 = (f32[112]{0:T(128)}, f32[112]{0:T(128)S(1)}, u32[]{:S(2)}) copy-start(f32[112]{0:T(128)S(1)} %compare_convert_fusion) | copy-start | bytes 1348
  41.8 26.0 %all-to-all-start = ((bf16[16,8,2048]{2,1,0:T(8,128)(2,1)}), bf16[16,8,2048]{2,1,0:T(8,128)(2,1)S(1)}, u32[]{:S(2)}, u32[]{:S(2)}) async-start(bf16[16,8,2048]{2,1,0:T(8,128)(2,1)} %pad_maximum_fusion), calls=%async_computation | async-start | bytes 1048576 | tf_op jit(solution)/shard_map/all_to_all | solution.py:64
  76.0 8.9 %collective-permute-start = (f32[4,8,1792]{2,1,0:T(8,128)}, f32[4,8,1792]{2,1,0:T(8,128)}, u32[]{:S(2)}, u32[]{:S(2)}) collective-permute-start(f32[4,8,1792]{2,1,0:T(8,128)} %pad_maximum_fusion.1), channel_id=1, source_target_pairs={{0,16},{32,48},{64,80},{96,112},{128,144},{160,176},{192,208},{224... | collective-permute-start | bytes 688136 | tf_op jit(solution)/shard_map/ppermute | solution.py:83
  91.8 43.9 %slice-start = ((s8[6422528]{0:T(1024)(128)(4,1)}), s8[2228224]{0:T(1024)(128)(4,1)S(1)}, s32[]{:S(2)}) async-start(s8[6422528]{0:T(1024)(128)(4,1)} %bitcast.342), calls=%async_computation.5 | async-start | bytes 4456448
  126.0 8.4 %collective-permute-start.1 = (f32[3,8,1792]{2,1,0:T(8,128)S(1)}, f32[3,8,1792]{2,1,0:T(8,128)S(1)}, u32[]{:S(2)}, u32[]{:S(2)}) collective-permute-start(f32[3,8,1792]{2,1,0:T(8,128)S(1)} %slice_add_fusion), channel_id=1, source_target_pairs={{16,32},{80,96},{144,160},{208,224},{17,33},{81,97},{145,161},{209... | collective-permute-start | bytes 516104 | tf_op jit(solution)/shard_map/ppermute | solution.py:88
  127.3 8.4 %collective-permute-start.2 = (f32[3,8,1792]{2,1,0:T(8,128)S(1)}, f32[3,8,1792]{2,1,0:T(8,128)S(1)}, u32[]{:S(2)}, u32[]{:S(2)}) collective-permute-start(f32[3,8,1792]{2,1,0:T(8,128)S(1)} %slice_add_fusion), channel_id=1, source_target_pairs={{48,32},{112,96},{176,160},{240,224},{49,33},{113,97},{177,161},{2... | collective-permute-start | bytes 516104 | tf_op jit(solution)/shard_map/ppermute | solution.py:88
  140.7 3.6 %collective-permute-start.3 = (f32[2,8,1792]{2,1,0:T(8,128)S(1)}, f32[2,8,1792]{2,1,0:T(8,128)S(1)}, u32[]{:S(2)}, u32[]{:S(2)}) collective-permute-start(f32[2,8,1792]{2,1,0:T(8,128)S(1)} %slice_add_fusion.1), channel_id=1, source_target_pairs={{32,64},{160,192},{33,65},{161,193},{34,66},{162,194},{35,67},{163... | collective-permute-start | bytes 344072 | tf_op jit(solution)/shard_map/ppermute | solution.py:88
  142.0 2.3 collective-permute-start.4
  147.1 1.4 collective-permute-start.5
  147.8 0.7 collective-permute-start.6
  156.9 1.3 collective-permute-start.7
  157.6 0.7 collective-permute-start.8
  163.9 2.0 collective-permute-start.10
  164.5 16.5 %collective-permute-start.9 = (bf16[2,8,1792]{2,1,0:T(8,128)(2,1)S(1)}, bf16[2,8,1792]{2,1,0:T(8,128)(2,1)S(1)}, u32[]{:S(2)}, u32[]{:S(2)}) collective-permute-start(bf16[2,8,1792]{2,1,0:T(8,128)(2,1)S(1)} %pad_maximum_fusion.4), channel_id=1, source_target_pairs={{64,32},{192,160},{65,33},{193,161},{66,34},{194,162},{67,35},{195... | collective-permute-start | bytes 172040 | tf_op jit(solution)/shard_map/ppermute | solution.py:123
  190.6 3.4 %collective-permute-start.11 = (bf16[3,8,1792]{2,1,0:T(8,128)(2,1)S(1)}, bf16[3,8,1792]{2,1,0:T(8,128)(2,1)S(1)}, u32[]{:S(2)}, u32[]{:S(2)}) collective-permute-start(bf16[3,8,1792]{2,1,0:T(8,128)(2,1)S(1)} %pad_maximum_fusion.3), channel_id=1, source_target_pairs={{32,16},{96,80},{160,144},{224,208},{33,17},{97,81},{161,145},{225... | collective-permute-start | bytes 258056 | tf_op jit(solution)/shard_map/ppermute | solution.py:123
  191.9 3.4 %collective-permute-start.12 = (bf16[3,8,1792]{2,1,0:T(8,128)(2,1)S(1)}, bf16[3,8,1792]{2,1,0:T(8,128)(2,1)S(1)}, u32[]{:S(2)}, u32[]{:S(2)}) collective-permute-start(bf16[3,8,1792]{2,1,0:T(8,128)(2,1)S(1)} %pad_maximum_fusion.3), channel_id=1, source_target_pairs={{32,48},{96,112},{160,176},{224,240},{33,49},{97,113},{161,177},{2... | collective-permute-start | bytes 258056 | tf_op jit(solution)/shard_map/ppermute | solution.py:123
  208.0 33.0 %copy-start.3 = (bf16[1,4,112,512]{3,2,1,0:T(8,128)(2,1)S(1)}, bf16[1,4,112,512]{3,2,1,0:T(8,128)(2,1)}, u32[]{:S(2)}) copy-start(bf16[1,4,112,512]{3,2,1,0:T(8,128)(2,1)} %param.10) | copy-start | bytes 1376260
  208.0 6.8 %collective-permute-start.13 = (bf16[4,8,1792]{2,1,0:T(8,128)(2,1)S(1)}, bf16[4,8,1792]{2,1,0:T(8,128)(2,1)S(1)}, u32[]{:S(2)}, u32[]{:S(2)}) collective-permute-start(bf16[4,8,1792]{2,1,0:T(8,128)(2,1)S(1)} %pad_maximum_fusion.2), channel_id=1, source_target_pairs={{16,0},{48,32},{80,64},{112,96},{144,128},{176,160},{208,192},{240... | collective-permute-start | bytes 344072 | tf_op jit(solution)/shard_map/ppermute | solution.py:118
  210.2 32.9 %all-to-all-start.2 = ((bf16[16,8,112]{2,1,0:T(8,128)(2,1)}), bf16[16,8,112]{2,1,0:T(8,128)(2,1)S(1)}, u32[]{:S(2)}, u32[]{:S(2)}) async-start(bf16[16,8,112]{2,1,0:T(8,128)(2,1)} %bitcast.341), calls=%async_computation.2 | async-start | bytes 65536 | tf_op jit(solution)/shard_map/all_to_all | solution.py:141
  243.1 19.4 %all-to-all-start.1 = ((bf16[16,112,128]{2,1,0:T(8,128)(2,1)}), bf16[16,112,128]{2,1,0:T(8,128)(2,1)S(1)}, u32[]{:S(2)}, u32[]{:S(2)}) async-start(bf16[16,112,128]{2,1,0:T(8,128)(2,1)} %bitcast.58), calls=%async_computation.1 | async-start | bytes 917504 | tf_op jit(solution)/shard_map/all_to_all | solution.py:137
  (12 other events, 161.2 us)
Sparse Core Ops, SparseCore 0:
  9.2 62.8 all-gather.5
  73.9 42.6 all-gather.7

commit v2 on v1

v2 whole, which is shorter than its diff:
```python
import functools

import jax
import jax.numpy as jnp
from jax import lax
from jax.experimental import pallas as pl
from jax.experimental.pallas import tpu as pltpu
from jax.sharding import PartitionSpec as P


BF = jnp.bfloat16
F32 = jnp.float32
VMEM_SPEC = pl.BlockSpec(memory_space=pltpu.VMEM)
SMEM_SPEC = pl.BlockSpec(memory_space=pltpu.SMEM)


def dot(a, b, ca, cb):
    return lax.dot_general(a, b, (((ca,), (cb,)), ((), ())), preferred_element_type=F32)


def call(body, outs, scalars, *args, scratch=()):
    return pl.pallas_call(
        body,
        out_shape=outs,
        in_specs=[SMEM_SPEC] + [VMEM_SPEC] * len(args),
        out_specs=jax.tree.map(lambda _: VMEM_SPEC, outs),
        scratch_shapes=list(scratch),
        compiler_params=pltpu.CompilerParams(vmem_limit_bytes=16 << 20),
    )(scalars, *args)


def row_mask(shape, live):
    return lax.broadcasted_iota(jnp.int32, shape, 1) < live


def one_pick(wanted, j):
    lanes = lax.broadcasted_iota(jnp.int32, wanted.shape, 1) + j * 128
    return jnp.where(wanted == lanes, 1.0, 0.0).astype(BF)


def picks_kernel(map_ref, pick_ref):
    slots, _, rows = pick_ref.shape


    @pl.loop(0, slots)
    def _(s):
        wanted = map_ref[s]
        for j in range(rows // 128):
            pick_ref[s, :, j * 128 : (j + 1) * 128] = one_pick(wanted, j)


def make_picks(wide, rows):
    slots, tile_len, _ = wide.shape
    return pl.pallas_call(
        picks_kernel,
        out_shape=jax.ShapeDtypeStruct((slots, tile_len, rows), BF),
        in_specs=[VMEM_SPEC],
        out_specs=VMEM_SPEC,
        compiler_params=pltpu.CompilerParams(vmem_limit_bytes=16 << 20),
        name="make_picks",
    )(wide)


def leaf_up_kernel(sc_ref, parts_ref, map_ref, acc_ref, base_ref, z_ref):
    slots, tile_len, _ = map_ref.shape
    groups, _ = parts_ref.shape[:2]
    rows = base_ref.shape[1]
    rows_dev, size = rows // (2 * groups), slots * tile_len
    total = parts_ref[0, :, :size].astype(F32)
    for k in range(1, groups):
        total = total + parts_ref[k, :, :size].astype(F32)
    for s in range(slots):
        z_ref[s] = total[:, s * tile_len : (s + 1) * tile_len]

    @pl.loop(0, slots)
    def _(s):
        z = z_ref[s].astype(BF)
        wanted = map_ref[s]
        for j in range(rows // 256):
            pick = jnp.concatenate([one_pick(wanted, 2 * j), one_pick(wanted, 2 * j + 1)], axis=1)
            acc_ref[s, :, j * 256 : (j + 1) * 256] = dot(z, pick, 1, 0).astype(BF)

    pieces = []
    for g in range(groups):
        for p in range(2):
            pieces.append(parts_ref[g, :, size + 128 * p : size + 128 * (p + 1)].astype(F32)[:, :rows_dev])
    base_ref[...] = jnp.concatenate(pieces, axis=1).astype(BF)


def up_kernel(height, sc_ref, base_ref, acc_a, acc_b, y_old, inv_ref, upd_ref, pick_ref, *outs):
    y_ref = outs[0]
    mask = row_mask(base_ref.shape, sc_ref[1])
    left = base_ref[...].astype(F32) - (acc_a[0].astype(F32) + acc_b[0].astype(F32))
    r = jnp.where(mask, left, 0.0).astype(BF)
    half = r.shape[1] // 2
    y = jnp.concatenate(
        [dot(r[:, :half], inv_ref[:half, :half], 1, 1), dot(r, inv_ref[half:, :], 1, 1)], axis=1
    )
    y = jnp.where(mask, y, 0.0).astype(BF)
    y_ref[...] = jnp.where(sc_ref[2] == height, y, y_old[...])
    if len(outs) > 1:
        acc_ref = outs[1]


        @pl.loop(0, acc_ref.shape[0])
        def _(s):
            z = dot(y, upd_ref[s], 1, 0).astype(BF)
            moved = dot(z, pick_ref[s], 1, 0)
            acc_ref[s] = (acc_a[s + 1].astype(F32) + acc_b[s + 1].astype(F32) + moved).astype(BF)


def down_kernel(height, sc_ref, y_ref, abo_a, abo_b, x_old, inv_ref, upd_ref, pick_ref, x_ref, out_ref):
    slots = out_ref.shape[0] - 1
    mask = row_mask(y_ref.shape, sc_ref[1])

    def pull(s, left):
        above = abo_a[s] + abo_b[s]
        out_ref[s + 1] = above
        tile = dot(above, pick_ref[s], 1, 1).astype(BF)
        return left - dot(tile, upd_ref[s], 1, 1)

    left = lax.fori_loop(0, slots, pull, y_ref[...].astype(F32))
    v = jnp.where(mask, left, 0.0).astype(BF)
    half = v.shape[1] // 2
    x = jnp.concatenate(
        [dot(v, inv_ref[:, :half], 1, 0), dot(v[:, half:], inv_ref[half:, half:], 1, 0)], axis=1
    )
    x = jnp.where(mask, x, 0.0).astype(BF)
    out_ref[0] = x
    x_ref[...] = jnp.where(sc_ref[2] == height, x, x_old[...])


def tiles_kernel(sc_ref, above_ref, pick_ref, tile_ref):
    slots, tile_len, _ = pick_ref.shape


    @pl.loop(0, slots)
    def _(s):
        here = pl.ds(pl.multiple_of(s * tile_len, 128), tile_len)
        tile_ref[:, here] = dot(above_ref[s], pick_ref[s], 1, 1).astype(BF)


def own_tiles_kernel(sc_ref, above_ref, map_ref, tile_ref):
    slots, tile_len, _ = map_ref.shape
    rows = above_ref.shape[2]

    @pl.loop(0, slots)
    def _(s):
        here = pl.ds(pl.multiple_of(s * tile_len, 128), tile_len)
        wanted = map_ref[s]
        above = above_ref[s]
        total = jnp.zeros((above.shape[0], tile_len), F32)
        for j in range(rows // 256):
            pick = jnp.concatenate([one_pick(wanted, 2 * j), one_pick(wanted, 2 * j + 1)], axis=1)
            total = total + dot(above[:, j * 256 : (j + 1) * 256], pick, 1, 1)
        tile_ref[:, here] = total.astype(BF)


def pack_kernel(sc_ref, inv_ref, upd_ref, fold_ref, half_ref, out_ref):
    col = sc_ref[4]
    low = out_ref.shape[1] - upd_ref.shape[0] * upd_ref.shape[2]
    tiles, spare = low // 128, fold_ref.shape[1] // 128
    for k in range(tiles):
        mine = inv_ref[:, k * 128 : (k + 1) * 128]
        m = tiles - 1 - k
        if m < spare:
            other = fold_ref[:, m * 128 : (m + 1) * 128]
        else:
            other = jnp.zeros_like(mine)
        own = jnp.where((col >= tiles) | (col >= k), 1, 0)
        keep = jnp.full(mine.shape, own, jnp.int32) == 1
        tile = jnp.where(keep, mine.astype(F32), other.astype(F32)).astype(BF)
        half_ref[:, k * 128 : (k + 1) * 128] = tile
        out_ref[:, k * 128 : (k + 1) * 128] = tile
    for s in range(upd_ref.shape[0]):
        size = upd_ref.shape[2]
        out_ref[:, low + s * size : low + (s + 1) * size] = upd_ref[s]


def join_kernel(sc_ref, upd_a, half_a, upd_b, half_b, out_a, out_b):
    for upd_ref, half_ref, out_ref in ((upd_a, half_a, out_a), (upd_b, half_b, out_b)):
        low, size = half_ref.shape[1], upd_ref.shape[2]
        out_ref[:, :low] = half_ref[...]
        for s in range(upd_ref.shape[0]):
            out_ref[:, low + s * size : low + (s + 1) * size] = upd_ref[s]


def place(col, first, chunk, inv_ref, upd_ref, blocks):
    count, rows_dev = chunk.shape[0], inv_ref.shape[0] // blocks
    low = chunk.shape[1] - upd_ref.shape[0] * upd_ref.shape[2]
    tiles, spare = low // 128, (inv_ref.shape[1] - low) // 128
    base = col * rows_dev + first
    other = (blocks - 1 - col) * rows_dev + first

    @pl.loop(0, count // 16)
    def _(i):
        at = pl.ds(pl.multiple_of(i * 16, 16), 16)
        here = pl.ds(pl.multiple_of(base + i * 16, 16), 16)
        there = pl.ds(pl.multiple_of(other + i * 16, 16), 16)
        for s in range(upd_ref.shape[0]):
            size = upd_ref.shape[2]
            upd_ref[s, here, :] = chunk[at, low + s * size : low + (s + 1) * size]

        @pl.when(col >= tiles)
        def _():
            inv_ref[here, :low] = chunk[at, :low]

        @pl.when(col < tiles)
        def _():
            for k in range(tiles):
                tile = chunk[at, k * 128 : (k + 1) * 128].astype(F32)
                own = jnp.full(tile.shape, jnp.where(col >= k, 1, 0), jnp.int32) == 1
                inv_ref[here, k * 128 : (k + 1) * 128] = jnp.where(own, tile, 0.0).astype(BF)
                m = tiles - 1 - k
                if m < spare:
                    to = low + m * 128
                    inv_ref[there, to : to + 128] = jnp.where(own, 0.0, tile).astype(BF)
            inv_ref[here, low:] = jnp.zeros((16, spare * 128), BF)


def gather_kernel(blocks, origins, firsts, sc_ref, *refs):
    chunks, (inv_ref, upd_ref) = refs[: len(origins)], refs[-2:]
    for chunk, (shift, flip), first in zip(chunks, origins, firsts):
        col = lax.rem(sc_ref[4] + 2 * shift + blocks, blocks)
        if flip:
            col = col + 1 - 2 * lax.rem(col, 2)
        place(col, first, chunk, inv_ref, upd_ref, blocks)


def leaf_fwd_kernel(sc_ref, r_ref, base_ref, inv_ref, upd_ref, y_ref, keep_ref, send_ref):
    rows_dev = inv_ref.shape[0]
    groups, part, _ = keep_ref.shape
    live_r = lax.broadcasted_iota(jnp.int32, r_ref.shape, 0) < sc_ref[0]
    r = jnp.where(live_r, r_ref[...].astype(F32), 0.0).astype(BF)
    mask = lax.broadcasted_iota(jnp.int32, y_ref.shape, 0) + sc_ref[4] * rows_dev < sc_ref[0]
    y = jnp.where(mask, dot(inv_ref[...], r, 1, 0), 0.0)
    y_ref[...] = y.astype(BF)
    turned = y.T.astype(BF)
    core = lax.rem(sc_ref[4], 2)
    slots, size = upd_ref.shape[0], upd_ref.shape[2]
    first = jnp.full((part, size), core, jnp.int32) == 0
    for s in range(slots):
        term = dot(turned, upd_ref[s], 1, 0)
        for g in range(groups):
            a = term[2 * g * part : (2 * g + 1) * part]
            b = term[(2 * g + 1) * part : (2 * g + 2) * part]
            keep_ref[g, :, s * size : (s + 1) * size] = jnp.where(first, a, b).astype(BF)
            send_ref[g, :, s * size : (s + 1) * size] = jnp.where(first, b, a).astype(BF)
    base = base_ref[...].astype(F32)
    base = jnp.concatenate([base, jnp.zeros((128 - rows_dev, base.shape[1]), F32)], axis=0).T
    first = jnp.full((part, 128), core, jnp.int32) == 0
    for g in range(groups):
        a = base[2 * g * part : (2 * g + 1) * part]
        b = base[(2 * g + 1) * part : (2 * g + 2) * part]
        keep_ref[g, :, slots * size :] = jnp.where(first, a, b).astype(BF)
        send_ref[g, :, slots * size :] = jnp.where(first, b, a).astype(BF)


def join_terms_kernel(sc_ref, keep_ref, got_ref, out_ref):
    groups, part, wide = keep_ref.shape
    size = wide - 128
    first = jnp.full((part, 128), lax.rem(sc_ref[4], 2), jnp.int32) == 0
    for g in range(groups):
        both = keep_ref[g, :, :size].astype(F32) + got_ref[g, :, :size].astype(F32)
        out_ref[g, :, :size] = both.astype(BF)
        own, other = keep_ref[g, :, size:].astype(F32), got_ref[g, :, size:].astype(F32)
        out_ref[g, :, size : size + 128] = jnp.where(first, own, other).astype(BF)
        out_ref[g, :, size + 128 :] = jnp.where(first, other, own).astype(BF)


def leaf_bwd_kernel(sc_ref, tile_ref, y_ref, upd_ref, inv_ref, x_ref, keep_ref, send_ref):
    rows_dev, width = y_ref.shape
    groups, part = keep_ref.shape[0], x_ref.shape[0]
    slots, size = upd_ref.shape[0], upd_ref.shape[2]
    left = y_ref[...].astype(F32)
    for s in range(slots):
        left = left - dot(upd_ref[s], tile_ref[:, s * size : (s + 1) * size], 1, 1)
    mask = lax.broadcasted_iota(jnp.int32, left.shape, 0) + sc_ref[4] * rows_dev < sc_ref[0]
    v = jnp.where(mask, left, 0.0).astype(BF)
    term = dot(inv_ref[...], v, 0, 0)
    core = lax.rem(sc_ref[4], 2)
    first = jnp.full((rows_dev, width), core, jnp.int32) == 0
    first_x = jnp.full((16, 128), core, jnp.int32) == 0
    x = x_ref[...].astype(F32)

    def block(at):
        piece = x[:, at * rows_dev : (at + 1) * rows_dev]
        piece = jnp.concatenate([piece, jnp.zeros((part, 128 - rows_dev), F32)], axis=1)
        return jnp.concatenate([piece, jnp.zeros((16 - part, 128), F32)], axis=0)

    for g in range(groups):
        a = term[2 * g * rows_dev : (2 * g + 1) * rows_dev]
        b = term[(2 * g + 1) * rows_dev : (2 * g + 2) * rows_dev]
        keep_ref[g, :rows_dev] = jnp.where(first, a, b).astype(BF)
        send_ref[g, :rows_dev] = jnp.where(first, b, a).astype(BF)
        xa, xb = block(2 * g), block(2 * g + 1)
        keep_ref[g, rows_dev:] = jnp.where(first_x, xa, xb).astype(BF)
        send_ref[g, rows_dev:] = jnp.where(first_x, xb, xa).astype(BF)


def merge_kernel(sc_ref, keep_ref, got_ref, out_ref):
    rows_dev = keep_ref.shape[1] - 16
    first = jnp.full((16, 128), lax.rem(sc_ref[4], 2), jnp.int32) == 0
    for g in range(keep_ref.shape[0]):
        both = keep_ref[g, :rows_dev].astype(F32) + got_ref[g, :rows_dev].astype(F32)
        out_ref[g, :rows_dev] = both.astype(BF)
        own, other = keep_ref[g, rows_dev:].astype(F32), got_ref[g, rows_dev:].astype(F32)
        out_ref[g, rows_dev : rows_dev + 16] = jnp.where(first, own, other).astype(BF)
        out_ref[g, rows_dev + 16 :] = jnp.where(first, other, own).astype(BF)


def final_kernel(sc_ref, in_ref, out_ref, wide_ref):
    rows_dev = out_ref.shape[1]
    groups, part = in_ref.shape[0], out_ref.shape[2] // (2 * in_ref.shape[0])
    total = in_ref[0, :rows_dev].astype(F32)
    for g in range(1, groups):
        total = total + in_ref[g, :rows_dev].astype(F32)
    mask = lax.broadcasted_iota(jnp.int32, total.shape, 0) + sc_ref[4] * rows_dev < sc_ref[0]
    out_ref[0] = jnp.where(mask, total, 0.0).astype(BF)
    for g in range(groups):
        for p in range(2):
            at, to = rows_dev + 16 * p, (2 * g + p) * part
            wide_ref[to : to + part] = in_ref[g, at : at + 16].astype(F32)[:part]
    out_ref[1] = wide_ref[...].T[:rows_dev].astype(BF)


def shards(
    right_sides, leaf_inverse, upper_inverse, leaf_update, upper_update, live_rows, tile_map
):
    leaf_count = lax.axis_size("leaf")
    col_count = lax.axis_size("col")
    depth = leaf_count.bit_length() - 1
    rows_dev = leaf_inverse.shape[1]
    rows = leaf_inverse.shape[2]
    width = right_sides.shape[3]
    part = width // col_count
    tile_len = tile_map.shape[3]
    leaf_id = lax.axis_index("leaf")
    col_id = lax.axis_index("col")

    node_level = jnp.zeros((), jnp.int32)
    for height in range(1, depth + 1):
        node_level = node_level + ((leaf_id % 2 ** (height - 1) == 0) & (leaf_id > 0)).astype(
            jnp.int32
        )
    scalars = jnp.stack([live_rows[0, 0], live_rows[0, 1], node_level, leaf_id % 2, col_id])

    wide_map = jnp.broadcast_to(tile_map[0, :, :, :, None], (2, depth, tile_len, 128))
    shape = jax.ShapeDtypeStruct
    blocks = col_count
    groups = blocks // 2
    low = rows // 2 + 128
    pairs = [(i, i ^ 1) for i in range(blocks)]
    members = [list(range(p, blocks, 2)) for p in range(2)]

    def along(x, step):
        return lax.ppermute(x, "col", [(i, (i + 2 * step) % blocks) for i in range(blocks)])

    def partner(x):
        return lax.ppermute(x, "col", pairs)

    own_upd = upper_update[0, : depth - 1]
    fold = lax.ppermute(
        upper_inverse[0, :, low:], "col", [(i, blocks - 1 - i) for i in range(blocks // 2, blocks)]
    )
    upd_a, upd_b = along(own_upd, 1), along(own_upd, -1)
    r_leaf = lax.all_gather(right_sides[0, 0], "col", axis=0, tiled=True)
    next_map = lax.ppermute(tile_map[0, 0], "leaf", [(i, i + 1) for i in range(0, leaf_count, 2)])
    fold, r_leaf, next_map = lax.optimization_barrier((fold, r_leaf, next_map))
    wide_next = jnp.broadcast_to(next_map[:, :, None], (depth, tile_len, 128))
    half, pack = call(
        pack_kernel,
        [shape((rows_dev, low), BF), shape((rows_dev, low + (depth - 1) * tile_len), BF)],
        scalars,
        upper_inverse[0],
        own_upd,
        fold,
    )
    half_a, half_b = along(half, 1), along(half, -1)
    y_leaf, keep, send = call(
        leaf_fwd_kernel,
        [shape((rows_dev, width), BF)] + [shape((groups, part, depth * tile_len + 128), BF)] * 2,
        scalars,
        r_leaf,
        right_sides[0, 1],
        leaf_inverse[0],
        leaf_update[0],
    )
    terms = call(
        join_terms_kernel,
        shape((groups, part, depth * tile_len + 256), BF),
        scalars,
        keep,
        partner(send),
    )
    swapped = lax.all_to_all(terms, "col", 0, 0, axis_index_groups=members)
    half_a, half_b, terms = lax.optimization_barrier((half_a, half_b, terms))
    ahead, behind = call(
        join_kernel, [shape(pack.shape, BF)] * 2, scalars, upd_a, half_a, upd_b, half_b
    )
    cut = rows_dev // 32 * 16 + 16
    chunks, origins, firsts = [pack, partner(pack)], [(0, False), (0, True)], [0, 0]
    for hop in range(1, groups // 2):
        if hop > 1:
            ahead, behind = along(ahead, 1), along(behind, -1)
        chunks += [ahead, behind, partner(ahead), partner(behind)]
        origins += [(-hop, False), (hop, False), (-hop, True), (hop, True)]
        firsts += [0] * 4
    acc, base_up = call(
        leaf_up_kernel,
        [shape((depth, part, rows), BF), shape((part, rows), BF)],
        scalars,
        swapped,
        wide_map[0],
        scratch=[pltpu.VMEM((depth, part, tile_len), F32)],
    )
    from_leaf = lax.ppermute(acc, "leaf", [(i, i + 1) for i in range(0, leaf_count, 2)])
    ahead, behind, acc = lax.optimization_barrier((ahead, behind, acc))
    far = groups // 2
    top, bottom = along(ahead[:cut], 1), along(behind[cut:], -1)
    last = [top, bottom, partner(top), partner(bottom)]
    last_origins = [(-far, False), (far, False), (-far, True), (far, True)]
    last_firsts = [0, cut, 0, cut]
    gathered = [shape((rows, rows), BF), shape((depth - 1, rows, tile_len), BF)]
    inv_up, upd_up = call(
        functools.partial(gather_kernel, blocks, origins, firsts), gathered, scalars, *chunks
    )
    inv_up, upd_up = pl.pallas_call(
        functools.partial(gather_kernel, blocks, last_origins, last_firsts),
        out_shape=gathered,
        in_specs=[SMEM_SPEC] + [VMEM_SPEC] * 6,
        out_specs=[VMEM_SPEC] * 2,
        input_output_aliases={5: 0, 6: 1},
        compiler_params=pltpu.CompilerParams(vmem_limit_bytes=16 << 20),
        name="gather_far",
    )(scalars, *last, inv_up, upd_up)

    pick_up = make_picks(wide_map[1, : depth - 1], rows)

    nodes = range(1, leaf_count)

    def level_of(node):
        return (node & -node).bit_length()

    y_up = jnp.zeros((part, rows), BF)
    for height in range(1, depth + 1):
        if height == 1:
            acc_a = acc
            acc_b = from_leaf
        else:
            step = 2 ** (height - 2)
            ups = [i for i in nodes if level_of(i) == height]
            acc_a = lax.ppermute(acc, "leaf", [(i - step, i) for i in ups])
            acc_b = lax.ppermute(acc, "leaf", [(i + step, i) for i in ups])
        if height == 2:
            acc_a, acc_b, next_pick = lax.optimization_barrier((acc_a, acc_b, next_pick))
        outs = [shape((part, rows), BF)]
        if height < depth:
            outs.append(shape((depth - height, part, rows), BF))
        y_up, *rest = call(
            functools.partial(up_kernel, height),
            outs,
            scalars,
            base_up,
            acc_a,
            acc_b,
            y_up,
            inv_up,
            upd_up,
            pick_up,
        )
        if rest:
            acc = rest[0]
        if height == 1:
            acc, wide_next = lax.optimization_barrier((acc, wide_next))
            next_pick = make_picks(wide_next, rows)

    x_up = jnp.zeros((part, rows), BF)
    abo_a = abo_b = jnp.zeros((1, part, rows), BF)
    for height in range(depth, 0, -1):
        x_up, above = call(
            functools.partial(down_kernel, height),
            [shape((part, rows), BF), shape((depth - height + 1, part, rows), BF)],
            scalars,
            y_up,
            abo_a,
            abo_b,
            x_up,
            inv_up,
            upd_up,
            pick_up,
        )
        if height == 1:
            sent = call(
                tiles_kernel, shape((part, depth * tile_len), BF), scalars, above, next_pick
            )
            got = lax.ppermute(sent, "leaf", [(i + 1, i) for i in range(0, leaf_count, 2)])
        else:
            step = 2 ** (height - 2)
            ups = [i for i in nodes if level_of(i) == height]
            abo_a = lax.ppermute(above, "leaf", [(i, i - step) for i in ups])
            abo_b = lax.ppermute(above, "leaf", [(i, i + step) for i in ups])

    tiles = call(own_tiles_kernel, shape((part, depth * tile_len), BF), scalars, above, wide_map[0])
    tiles = jnp.where(leaf_id % 2 == 1, tiles, got)
    tiles = lax.all_gather(tiles, "col", axis=0, tiled=True)
    keep, send = call(
        leaf_bwd_kernel,
        [shape((groups, rows_dev + 16, width), BF)] * 2,
        scalars,
        tiles,
        y_leaf,
        leaf_update[0],
        leaf_inverse[0],
        x_up,
    )
    merged = call(
        merge_kernel, shape((groups, rows_dev + 32, width), BF), scalars, keep, partner(send)
    )
    swapped = lax.all_to_all(merged, "col", 0, 0, axis_index_groups=members)
    return call(
        final_kernel,
        shape((2, rows_dev, width), BF),
        scalars,
        swapped,
        scratch=[pltpu.VMEM((width, 128), F32)],
    )[None]


def solution(mesh):
    placed = (
        P("leaf", None, "col", None),
        P("leaf", "col", None),
        P("leaf", "col", None),
        P("leaf", None, "col", None),
        P("leaf", None, "col", None),
        P("leaf", None),
        P("leaf", None, None, None),
    )

    return jax.shard_map(
        shards, mesh=mesh, in_specs=placed, out_specs=P("leaf", None, "col", None), check_vma=False
    )
```

time: 275 us -> 225 us (0.82); the launches traced: 270 us -> 223 us
  matrix products: 75.2 us -> 0 us
  Pallas kernels: 0 us -> 48.1 us
  waiting for transfers between devices: 82.6 us -> 61.2 us
  starting transfers between devices: 30.2 us -> 50.5 us
  between operations: 14.1 us -> 0.42 us
  other arithmetic: 12.3 us -> 0.01 us
  blocking collectives: 43.8 us -> 53 us
    dot_general x43 -> x0, matrix products: 75.2 us -> none  [dot(): lax.dot_general(a, b, (((ca,), (cb,)), ((), ())), preferred_element_type=...]
    pallas_call x0 -> x22, Pallas kernels: none -> 48.1 us  [the longest x19 44.4 us: call(): pl.pallas_call(body, out_shape=outs, in_specs=[SMEM_SPEC] + [VMEM_SPEC] *...]
    ppermute x13 -> x36, waiting for transfers between devices: 25.9 us -> 57.4 us  [the longest x10 33.9 us: along(): lax.ppermute(x, 'col', [(i, (i + 2 * step) % blocks) for i in range(block...]
    ppermute x13 -> x36, starting transfers between devices: 13.4 us -> 39.9 us  [the longest x10 20.5 us: along(): lax.ppermute(x, 'col', [(i, (i + 2 * step) % blocks) for i in range(block...]
    all_gather x2 -> x0, waiting for transfers between devices: 24.8 us -> none  [the longest x1 24.8 us: shards(): lax.all_gather(upper_update[0, :depth - 1], 'col', axis=1, tiled=True)]
    all_to_all x3 -> x1, waiting for transfers between devices: 28.6 us -> 3.76 us  [shards(): swapped = lax.all_to_all(terms, 'col', 0, 0, axis_index_groups=members)]
    all_to_all x0 -> x1, blocking collectives: none -> 16.8 us  [shards(): swapped = lax.all_to_all(merged, 'col', 0, 0, axis_index_groups=members)]
    eq x1 -> x0, other arithmetic: 6.71 us -> none  [shards(): tile_map[0][:, :, :, None]]
  transfers between devices with their start and end apart: 19 -> 38, of which waited for: 10 -> 17; matrix products, arithmetic and copies ran while one was open for 16% -> 3% of each run, Pallas kernels for 0% -> 8%
where the time goes in v2:
time: 225 us; the launch traced here: 223 us
  waiting for transfers between devices  61.2 us (27%)
  blocking collectives  53 us (24%)
  starting transfers between devices  50.5 us (22%)
  Pallas kernels  48.1 us (21%)
  local copies, waits for them, and re-layouts  10 us (4%)
    pallas_call x19, Pallas kernels, call(): pl.pallas_call(body, out_shape=outs, in_specs=[SMEM_SPEC] + [VMEM_SPEC] *...  44.4 us
    ppermute x10, waiting for transfers between devices, along(): lax.ppermute(x, 'col', [(i, (i + 2 * step) % blocks) for i in range(block...  33.9 us
    ppermute x10, starting transfers between devices, along(): lax.ppermute(x, 'col', [(i, (i + 2 * step) % blocks) for i in range(block...  20.5 us
    all_gather x1, blocking collectives, shards(): r_leaf = lax.all_gather(right_sides[0, 0], 'col', axis=0, tiled=True)  19.2 us
    all_gather x1, blocking collectives, shards(): tiles = lax.all_gather(tiles, 'col', axis=0, tiled=True)  17 us
    all_to_all x1, blocking collectives, shards(): swapped = lax.all_to_all(merged, 'col', 0, 0, axis_index_groups=members)  16.8 us
    ppermute x3, waiting for transfers between devices, shards(): abo_a = lax.ppermute(above, 'leaf', [(i, i - step) for i in ups])  14.6 us
    all_to_all x1, starting transfers between devices, shards(): swapped = lax.all_to_all(terms, 'col', 0, 0, axis_index_groups=members)  7.43 us
  transfers between devices with their start and end apart: 38, of which 17 were waited for; matrix products, arithmetic and copies ran while one was open for 3% of the time, Pallas kernels for 8%

profile of v2, /device:TPU:4, one launch (start us, length us, event | category | flops | bytes accessed | tf_op | source)
XLA Modules:
  0.0 223.2 jit_solution(9785439377245897214)
XLA Ops:
  3.0 4.0 %collective-permute-start.6 = (bf16[3,112,512]{2,1,0:T(8,128)(2,1)S(1)}, bf16[3,112,512]{2,1,0:T(8,128)(2,1)S(1)}, u32[]{:S(2)}, u32[]{:S(2)}) collective-permute-start(bf16[3,112,512]{2,1,0:T(8,128)(2,1)S(1)} %slice_bitcast_fusion.upd_ref), channel_id=1, source_target_pairs={{0,14},{1,15},{2,0},{3,1},{4,2},{5,3},{6,4},{7,5},{8,6},{9,7},{10,... | collective-permute-start | bytes 1032200 | tf_op jit(solution)/shard_map/ppermute | solution.py:357
  7.7 3.1 %collective-permute-start.1 = (s32[4,512]{1,0:T(4,128)S(1)}, s32[4,512]{1,0:T(4,128)S(1)}, u32[]{:S(2)}, u32[]{:S(2)}) collective-permute-start(s32[4,512]{1,0:T(4,128)S(1)} %slice_bitcast_fusion.4), channel_id=1, source_target_pairs={{0,16},{32,48},{64,80},{96,112},{128,144},{160,176},{192,208},{224... | collective-permute-start | bytes 24584 | tf_op jit(solution)/shard_map/ppermute | solution.py:368
  13.8 19.2 %all-gather = bf16[1,1,1792,128]{3,2,1,0:T(8,128)(2,1)S(1)} all-gather(bf16[1,1,112,128]{3,2,1,0:T(8,128)(2,1)S(1)} %get-tuple-element.90), channel_id=2, replica_groups=mesh['leaf'=16,'col'=16] {'col'}, dimensions={2}, use_global_device_ids=true | all-gather | bytes 487424 | tf_op jit(solution)/shard_map/all_gather | solution.py:367
  40.7 3.0 %collective-permute-start.4 = (bf16[112,1024]{1,0:T(8,128)(2,1)S(1)}, bf16[112,1024]{1,0:T(8,128)(2,1)S(1)}, u32[]{:S(2)}, u32[]{:S(2)}) collective-permute-start(bf16[112,1024]{1,0:T(8,128)(2,1)S(1)} %get-tuple-element.52), channel_id=1, source_target_pairs={{0,2},{1,3},{2,4},{3,5},{4,6},{5,7},{6,8},{7,9},{8,10},{9,11},{10,... | collective-permute-start | bytes 688136 | tf_op jit(solution)/shard_map/ppermute | solution.py:357
  45.3 4.5 %collective-permute-done.4.half_a = bf16[112,1024]{1,0:T(8,128)(2,1)S(1)} collective-permute-done((bf16[112,1024]{1,0:T(8,128)(2,1)S(1)}, bf16[112,1024]{1,0:T(8,128)(2,1)S(1)}, u32[]{:S(2)}, u32[]{:S(2)}) %collective-permute-start.4) | collective-permute-done | bytes 229408 | tf_op jit(solution)/shard_map/ppermute | solution.py:357
  56.0 12.2 %collective-permute-done.7.refs_6_ = bf16[112,2560]{1,0:T(8,128)(2,1)} collective-permute-done((bf16[112,2560]{1,0:T(8,128)(2,1)}, bf16[112,2560]{1,0:T(8,128)(2,1)}, u32[]{:S(2)}, u32[]{:S(2)}) %collective-permute-start.7) | collective-permute-done | bytes 573472 | tf_op jit(solution)/shard_map/ppermute | solution.py:357
  71.5 7.4 %all-to-all-start = ((bf16[8,8,2304]{2,1,0:T(8,128)(2,1)}), bf16[8,8,2304]{2,1,0:T(8,128)(2,1)S(1)}, u32[]{:S(2)}, u32[]{:S(2)}) async-start(bf16[8,8,2304]{2,1,0:T(8,128)(2,1)} %shard_map.74), calls=%async_computation | async-start | bytes 589824 | tf_op jit(solution)/shard_map/all_to_all | solution.py:396
  79.4 3.3 %collective-permute-done.8.refs_10_ = bf16[112,2560]{1,0:T(8,128)(2,1)S(1)} collective-permute-done((bf16[112,2560]{1,0:T(8,128)(2,1)}, bf16[112,2560]{1,0:T(8,128)(2,1)S(1)}, u32[]{:S(2)}, u32[]{:S(2)}) %collective-permute-start.8) | collective-permute-done | bytes 573472 | tf_op jit(solution)/shard_map/ppermute | solution.py:357
  82.7 4.2 %collective-permute-done.10.refs_11_ = bf16[112,2560]{1,0:T(8,128)(2,1)S(1)} collective-permute-done((bf16[112,2560]{1,0:T(8,128)(2,1)}, bf16[112,2560]{1,0:T(8,128)(2,1)S(1)}, u32[]{:S(2)}, u32[]{:S(2)}) %collective-permute-start.10) | collective-permute-done | bytes 573472 | tf_op jit(solution)/shard_map/ppermute | solution.py:357
  87.0 3.8 %all-to-all-done.parts_ref = bf16[8,8,2304]{2,1,0:T(8,128)(2,1)S(1)} async-done(((bf16[8,8,2304]{2,1,0:T(8,128)(2,1)}), bf16[8,8,2304]{2,1,0:T(8,128)(2,1)S(1)}, u32[]{:S(2)}, u32[]{:S(2)}) %all-to-all-start) | async-done | bytes 294944 | tf_op jit(solution)/shard_map/all_to_all | solution.py:396
  93.1 5.1 %collective-permute-start.12 = (bf16[64,2560]{1,0:T(8,128)(2,1)S(1)}, bf16[64,2560]{1,0:T(8,128)(2,1)S(1)}, u32[]{:S(2)}, u32[]{:S(2)}) collective-permute-start(bf16[64,2560]{1,0:T(8,128)(2,1)S(1)} %slice.42), channel_id=1, source_target_pairs={{0,2},{1,3},{2,4},{3,5},{4,6},{5,7},{6,8},{7,9},{8,10},{9,11},{10,... | collective-permute-start | bytes 983048 | tf_op jit(solution)/shard_map/ppermute | solution.py:357
  98.8 4.8 %collective-permute-done.12.refs_0_ = bf16[64,2560]{1,0:T(8,128)(2,1)S(1)} collective-permute-done((bf16[64,2560]{1,0:T(8,128)(2,1)S(1)}, bf16[64,2560]{1,0:T(8,128)(2,1)S(1)}, u32[]{:S(2)}, u32[]{:S(2)}) %collective-permute-start.12) | collective-permute-done | bytes 327712 | tf_op jit(solution)/shard_map/ppermute | solution.py:357
  103.7 3.1 %collective-permute-done.13.refs_1_ = bf16[48,2560]{1,0:T(8,128)(2,1)S(1)} collective-permute-done((bf16[48,2560]{1,0:T(8,128)(2,1)S(1)}, bf16[48,2560]{1,0:T(8,128)(2,1)S(1)}, u32[]{:S(2)}, u32[]{:S(2)}) %collective-permute-start.13) | collective-permute-done | bytes 245792 | tf_op jit(solution)/shard_map/ppermute | solution.py:357
  106.8 3.1 %collective-permute-start.11 = (bf16[4,8,1792]{2,1,0:T(8,128)(2,1)S(1)}, bf16[4,8,1792]{2,1,0:T(8,128)(2,1)S(1)}, u32[]{:S(2)}, u32[]{:S(2)}) collective-permute-start(bf16[4,8,1792]{2,1,0:T(8,128)(2,1)S(1)} %get-tuple-element.58.acc_a), channel_id=1, source_target_pairs={{0,16},{32,48},{64,80},{96,112},{128,144},{160,176},{192,208},{224... | collective-permute-start | bytes 344072 | tf_op jit(solution)/shard_map/ppermute | solution.py:417
  111.4 5.2 %shard_map.78 = (bf16[1792,1792]{1,0:T(8,128)(2,1)S(1)}, bf16[3,1792,512]{2,1,0:T(8,128)(2,1)S(1)}) custom-call(s32[5]{0:T(128)S(1)} %stack.15.sc_ref, bf16[112,2560]{1,0:T(8,128)(2,1)S(1)} %get-tuple-element.61.refs_0_, bf16[112,2560]{1,0:T(8,128)(2,1)} %collective-permute-done.16.refs_1_, bf16[112,2560]{1,0:T(8,128)(2,1)} %get-tuple-element.55.refs_2_, ...), custom_call_target="tpu_custom_call" | custom-call | tf_op jit(solution)/shard_map/pallas_call | solution.py:22
  117.6 3.9 %shard_map.79 = (bf16[8,1792]{1,0:T(8,128)(2,1)S(1)}, bf16[3,8,1792]{2,1,0:T(8,128)(2,1)S(1)}) custom-call(s32[5]{0:T(128)S(1)} %stack.15.sc_ref, bf16[8,1792]{1,0:T(8,128)(2,1)S(1)} %get-tuple-element.50.base_ref, bf16[4,8,1792]{2,1,0:T(8,128)(2,1)S(1)} %get-tuple-element.58.acc_a, bf16[4,8,1792]{2,1,0:T(8,128)(2,1)S(1)} %collective-permute-done.11.acc_b, ...), custom_call_target="tpu_custom_call" | custom-call | tf_op jit(solution)/shard_map/pallas_call | solution.py:22
  129.7 3.3 %shard_map.80 = (bf16[8,1792]{1,0:T(8,128)(2,1)S(1)}, bf16[2,8,1792]{2,1,0:T(8,128)(2,1)S(1)}) custom-call(s32[5]{0:T(128)S(1)} %stack.15.sc_ref, bf16[8,1792]{1,0:T(8,128)(2,1)S(1)} %get-tuple-element.50.base_ref, bf16[3,8,1792]{2,1,0:T(8,128)(2,1)S(1)} %collective-permute-done.23.acc_a, bf16[3,8,1792]{2,1,0:T(8,128)(2,1)S(1)} %collective-permute-done.24.acc_b, ...), custom_call_target="tpu_custom_call" | custom-call | tf_op jit(solution)/shard_map/pallas_call | solution.py:22
  148.8 14.0 %collective-permute-done.31.abo_a = bf16[2,8,1792]{2,1,0:T(8,128)(2,1)S(1)} collective-permute-done((bf16[2,8,1792]{2,1,0:T(8,128)(2,1)S(1)}, bf16[2,8,1792]{2,1,0:T(8,128)(2,1)S(1)}, u32[]{:S(2)}, u32[]{:S(2)}) %collective-permute-start.31) | collective-permute-done | bytes 57376 | tf_op jit(solution)/shard_map/ppermute | solution.py:501
  162.9 3.7 %shard_map.85 = (bf16[8,1792]{1,0:T(8,128)(2,1)S(1)}, bf16[3,8,1792]{2,1,0:T(8,128)(2,1)S(1)}) custom-call(s32[5]{0:T(128)S(1)} %stack.15.sc_ref, bf16[8,1792]{1,0:T(8,128)(2,1)S(1)} %shard_map.82.y_ref, bf16[2,8,1792]{2,1,0:T(8,128)(2,1)S(1)} %collective-permute-done.31.abo_a, bf16[2,8,1792]{2,1,0:T(8,128)(2,1)S(1)} %collective-permute-done.32.abo_b, ...), custom_call_target="tpu_custom_call" | custom-call | tf_op jit(solution)/shard_map/pallas_call | solution.py:22
  171.2 4.8 %shard_map.86 = (bf16[8,1792]{1,0:T(8,128)(2,1)S(1)}, bf16[4,8,1792]{2,1,0:T(8,128)(2,1)S(1)}) custom-call(s32[5]{0:T(128)S(1)} %stack.15.sc_ref, bf16[8,1792]{1,0:T(8,128)(2,1)S(1)} %shard_map.82.y_ref, bf16[3,8,1792]{2,1,0:T(8,128)(2,1)S(1)} %collective-permute-done.33.abo_a, bf16[3,8,1792]{2,1,0:T(8,128)(2,1)S(1)} %collective-permute-done.34.abo_b, ...), custom_call_target="tpu_custom_call" | custom-call | tf_op jit(solution)/shard_map/pallas_call | solution.py:22
  176.1 2.9 %shard_map.88 = bf16[8,2048]{1,0:T(8,128)(2,1)S(1)} custom-call(s32[5]{0:T(128)S(1)} %stack.15.sc_ref, bf16[4,8,1792]{2,1,0:T(8,128)(2,1)S(1)} %get-tuple-element.83.above_ref, bf16[4,512,1792]{2,1,0:T(8,128)(2,1)S(1)} %make_picks.3.pick_ref), custom_call_target="tpu_custom_call" | custom-call | tf_op jit(solution)/shard_map/pallas_call | solution.py:22
  180.2 2.9 %shard_map.87 = bf16[8,2048]{1,0:T(8,128)(2,1)S(1)} custom-call(s32[5]{0:T(128)S(1)} %stack.15.sc_ref, bf16[4,8,1792]{2,1,0:T(8,128)(2,1)S(1)} %get-tuple-element.83.above_ref, s32[4,512,128]{2,1,0:T(8,128)S(1)} %broadcast_in_dim.23.map_ref), custom_call_target="tpu_custom_call" | custom-call | tf_op jit(solution)/shard_map/pallas_call | solution.py:22
  184.8 17.0 %all_gather.7.tile_ref = bf16[128,2048]{1,0:T(8,128)(2,1)S(1)} all-gather(bf16[8,2048]{1,0:T(8,128)(2,1)S(1)} %broadcast_select_fusion), channel_id=1, replica_groups=mesh['leaf'=16,'col'=16] {'col'}, dimensions={0}, use_global_device_ids=true | all-gather | bytes 557056 | tf_op jit(solution)/shard_map/all_gather | solution.py:506
  205.2 16.8 %all_to_all.10.in_ref = bf16[8,144,128]{2,1,0:T(8,128)(2,1)S(1)} all-to-all(bf16[8,144,128]{2,1,0:T(8,128)(2,1)S(1)} %shard_map.90), channel_id=1, replica_groups={{0,2,4,6,8,10,12,14},{1,3,5,7,9,11,13,15},{16,18,20,22,24,26,28,30},{17..., dimensions={0} | all-to-all | bytes 589824 | tf_op jit(solution)/shard_map/all_to_all | solution.py:520
  (104 shorter events, 67.4 us)
Async XLA Ops:
  1.0 50.1 %collective-permute-start.3 = (bf16[3,112,512]{2,1,0:T(8,128)(2,1)S(1)}, bf16[3,112,512]{2,1,0:T(8,128)(2,1)S(1)}, u32[]{:S(2)}, u32[]{:S(2)}) collective-permute-start(bf16[3,112,512]{2,1,0:T(8,128)(2,1)S(1)} %slice_bitcast_fusion.upd_ref), channel_id=1, source_target_pairs={{0,2},{1,3},{2,4},{3,5},{4,6},{5,7},{6,8},{7,9},{8,10},{9,11},{10,... | collective-permute-start | bytes 1032200 | tf_op jit(solution)/shard_map/ppermute | solution.py:357
  3.0 48.1 %collective-permute-start.6 = (bf16[3,112,512]{2,1,0:T(8,128)(2,1)S(1)}, bf16[3,112,512]{2,1,0:T(8,128)(2,1)S(1)}, u32[]{:S(2)}, u32[]{:S(2)}) collective-permute-start(bf16[3,112,512]{2,1,0:T(8,128)(2,1)S(1)} %slice_bitcast_fusion.upd_ref), channel_id=1, source_target_pairs={{0,14},{1,15},{2,0},{3,1},{4,2},{5,3},{6,4},{7,5},{8,6},{9,7},{10,... | collective-permute-start | bytes 1032200 | tf_op jit(solution)/shard_map/ppermute | solution.py:357
  7.7 27.9 %collective-permute-start.1 = (s32[4,512]{1,0:T(4,128)S(1)}, s32[4,512]{1,0:T(4,128)S(1)}, u32[]{:S(2)}, u32[]{:S(2)}) collective-permute-start(s32[4,512]{1,0:T(4,128)S(1)} %slice_bitcast_fusion.4), channel_id=1, source_target_pairs={{0,16},{32,48},{64,80},{96,112},{128,144},{160,176},{192,208},{224... | collective-permute-start | bytes 24584 | tf_op jit(solution)/shard_map/ppermute | solution.py:368
  11.8 23.8 %collective-permute-start = (bf16[112,768]{1,0:T(8,128)(2,1)S(1)}, bf16[112,768]{1,0:T(8,128)(2,1)S(1)}, u32[]{:S(2)}, u32[]{:S(2)}) collective-permute-start(bf16[112,768]{1,0:T(8,128)(2,1)S(1)} %slice_bitcast_fusion.1), channel_id=1, source_target_pairs={{8,7},{9,6},{10,5},{11,4},{12,3},{13,2},{14,1},{15,0},{24,23},{25,... | collective-permute-start | bytes 516104 | tf_op jit(solution)/shard_map/ppermute | solution.py:363
  40.7 9.1 %collective-permute-start.4 = (bf16[112,1024]{1,0:T(8,128)(2,1)S(1)}, bf16[112,1024]{1,0:T(8,128)(2,1)S(1)}, u32[]{:S(2)}, u32[]{:S(2)}) collective-permute-start(bf16[112,1024]{1,0:T(8,128)(2,1)S(1)} %get-tuple-element.52), channel_id=1, source_target_pairs={{0,2},{1,3},{2,4},{3,5},{4,6},{5,7},{6,8},{7,9},{8,10},{9,11},{10,... | collective-permute-start | bytes 688136 | tf_op jit(solution)/shard_map/ppermute | solution.py:357
  52.8 15.4 %collective-permute-start.7 = (bf16[112,2560]{1,0:T(8,128)(2,1)}, bf16[112,2560]{1,0:T(8,128)(2,1)}, u32[]{:S(2)}, u32[]{:S(2)}) collective-permute-start(bf16[112,2560]{1,0:T(8,128)(2,1)} %get-tuple-element.55.refs_2_), channel_id=1, source_target_pairs={{0,2},{1,3},{2,4},{3,5},{4,6},{5,7},{6,8},{7,9},{8,10},{9,11},{10,... | collective-permute-start | bytes 1720328 | tf_op jit(solution)/shard_map/ppermute | solution.py:357
  54.4 15.2 %collective-permute-start.9 = (bf16[112,2560]{1,0:T(8,128)(2,1)}, bf16[112,2560]{1,0:T(8,128)(2,1)}, u32[]{:S(2)}, u32[]{:S(2)}) collective-permute-start(bf16[112,2560]{1,0:T(8,128)(2,1)} %get-tuple-element.56.refs_3_), channel_id=1, source_target_pairs={{0,14},{1,15},{2,0},{3,1},{4,2},{5,3},{6,4},{7,5},{8,6},{9,7},{10,... | collective-permute-start | bytes 1720328 | tf_op jit(solution)/shard_map/ppermute | solution.py:357
  68.2 14.5 %collective-permute-start.8 = (bf16[112,2560]{1,0:T(8,128)(2,1)}, bf16[112,2560]{1,0:T(8,128)(2,1)S(1)}, u32[]{:S(2)}, u32[]{:S(2)}) collective-permute-start(bf16[112,2560]{1,0:T(8,128)(2,1)} %collective-permute-done.7.refs_6_), channel_id=1, source_target_pairs={{0,2},{1,3},{2,4},{3,5},{4,6},{5,7},{6,8},{7,9},{8,10},{9,11},{10,... | collective-permute-start | bytes 1720328 | tf_op jit(solution)/shard_map/ppermute | solution.py:357
  69.6 17.4 %collective-permute-start.10 = (bf16[112,2560]{1,0:T(8,128)(2,1)}, bf16[112,2560]{1,0:T(8,128)(2,1)S(1)}, u32[]{:S(2)}, u32[]{:S(2)}) collective-permute-start(bf16[112,2560]{1,0:T(8,128)(2,1)} %collective-permute-done.9.refs_7_), channel_id=1, source_target_pairs={{0,14},{1,15},{2,0},{3,1},{4,2},{5,3},{6,4},{7,5},{8,6},{9,7},{10,... | collective-permute-start | bytes 1720328 | tf_op jit(solution)/shard_map/ppermute | solution.py:357
  71.5 21.6 %collective-permute-start.16 = (bf16[112,2560]{1,0:T(8,128)(2,1)S(1)}, bf16[112,2560]{1,0:T(8,128)(2,1)}, u32[]{:S(2)}, u32[]{:S(2)}) collective-permute-start(bf16[112,2560]{1,0:T(8,128)(2,1)S(1)} %get-tuple-element.61.refs_0_), channel_id=1, source_target_pairs={{0,1},{1,0},{2,3},{3,2},{4,5},{5,4},{6,7},{7,6},{8,9},{9,8},{10,11... | collective-permute-start | bytes 1720328 | tf_op jit(solution)/shard_map/ppermute | solution.py:360
  71.5 19.2 %all-to-all-start = ((bf16[8,8,2304]{2,1,0:T(8,128)(2,1)}), bf16[8,8,2304]{2,1,0:T(8,128)(2,1)S(1)}, u32[]{:S(2)}, u32[]{:S(2)}) async-start(bf16[8,8,2304]{2,1,0:T(8,128)(2,1)} %shard_map.74), calls=%async_computation | async-start | bytes 589824 | tf_op jit(solution)/shard_map/all_to_all | solution.py:396
  78.9 19.3 %collective-permute-start.17 = (bf16[112,2560]{1,0:T(8,128)(2,1)}, bf16[112,2560]{1,0:T(8,128)(2,1)}, u32[]{:S(2)}, u32[]{:S(2)}) collective-permute-start(bf16[112,2560]{1,0:T(8,128)(2,1)} %get-tuple-element.55.refs_2_), channel_id=1, source_target_pairs={{0,1},{1,0},{2,3},{3,2},{4,5},{5,4},{6,7},{7,6},{8,9},{9,8},{10,11... | collective-permute-start | bytes 1720328 | tf_op jit(solution)/shard_map/ppermute | solution.py:360
  79.1 19.1 %collective-permute-start.18 = (bf16[112,2560]{1,0:T(8,128)(2,1)}, bf16[112,2560]{1,0:T(8,128)(2,1)}, u32[]{:S(2)}, u32[]{:S(2)}) collective-permute-start(bf16[112,2560]{1,0:T(8,128)(2,1)} %get-tuple-element.56.refs_3_), channel_id=1, source_target_pairs={{0,1},{1,0},{2,3},{3,2},{4,5},{5,4},{6,7},{7,6},{8,9},{9,8},{10,11... | collective-permute-start | bytes 1720328 | tf_op jit(solution)/shard_map/ppermute | solution.py:360
  82.7 16.0 %collective-permute-start.19 = (bf16[112,2560]{1,0:T(8,128)(2,1)}, bf16[112,2560]{1,0:T(8,128)(2,1)}, u32[]{:S(2)}, u32[]{:S(2)}) collective-permute-start(bf16[112,2560]{1,0:T(8,128)(2,1)} %collective-permute-done.7.refs_6_), channel_id=1, source_target_pairs={{0,1},{1,0},{2,3},{3,2},{4,5},{5,4},{6,7},{7,6},{8,9},{9,8},{10,11... | collective-permute-start | bytes 1720328 | tf_op jit(solution)/shard_map/ppermute | solution.py:360
  87.0 19.8 %collective-permute-start.20 = (bf16[112,2560]{1,0:T(8,128)(2,1)}, bf16[112,2560]{1,0:T(8,128)(2,1)}, u32[]{:S(2)}, u32[]{:S(2)}) collective-permute-start(bf16[112,2560]{1,0:T(8,128)(2,1)} %collective-permute-done.9.refs_7_), channel_id=1, source_target_pairs={{0,1},{1,0},{2,3},{3,2},{4,5},{5,4},{6,7},{7,6},{8,9},{9,8},{10,11... | collective-permute-start | bytes 1720328 | tf_op jit(solution)/shard_map/ppermute | solution.py:360
  93.1 10.6 %collective-permute-start.12 = (bf16[64,2560]{1,0:T(8,128)(2,1)S(1)}, bf16[64,2560]{1,0:T(8,128)(2,1)S(1)}, u32[]{:S(2)}, u32[]{:S(2)}) collective-permute-start(bf16[64,2560]{1,0:T(8,128)(2,1)S(1)} %slice.42), channel_id=1, source_target_pairs={{0,2},{1,3},{2,4},{3,5},{4,6},{5,7},{6,8},{7,9},{8,10},{9,11},{10,... | collective-permute-start | bytes 983048 | tf_op jit(solution)/shard_map/ppermute | solution.py:357
  98.2 13.2 %collective-permute-start.21 = (bf16[112,2560]{1,0:T(8,128)(2,1)S(1)}, bf16[112,2560]{1,0:T(8,128)(2,1)S(1)}, u32[]{:S(2)}, u32[]{:S(2)}) collective-permute-start(bf16[112,2560]{1,0:T(8,128)(2,1)S(1)} %collective-permute-done.8.refs_10_), channel_id=1, source_target_pairs={{0,1},{1,0},{2,3},{3,2},{4,5},{5,4},{6,7},{7,6},{8,9},{9,8},{10,11... | collective-permute-start | bytes 1720328 | tf_op jit(solution)/shard_map/ppermute | solution.py:360
  98.2 13.2 %collective-permute-start.22 = (bf16[112,2560]{1,0:T(8,128)(2,1)S(1)}, bf16[112,2560]{1,0:T(8,128)(2,1)S(1)}, u32[]{:S(2)}, u32[]{:S(2)}) collective-permute-start(bf16[112,2560]{1,0:T(8,128)(2,1)S(1)} %collective-permute-done.10.refs_11_), channel_id=1, source_target_pairs={{0,1},{1,0},{2,3},{3,2},{4,5},{5,4},{6,7},{7,6},{8,9},{9,8},{10,11... | collective-permute-start | bytes 1720328 | tf_op jit(solution)/shard_map/ppermute | solution.py:360
  98.7 8.0 %collective-permute-start.13 = (bf16[48,2560]{1,0:T(8,128)(2,1)S(1)}, bf16[48,2560]{1,0:T(8,128)(2,1)S(1)}, u32[]{:S(2)}, u32[]{:S(2)}) collective-permute-start(bf16[48,2560]{1,0:T(8,128)(2,1)S(1)} %slice.43), channel_id=1, source_target_pairs={{0,14},{1,15},{2,0},{3,1},{4,2},{5,3},{6,4},{7,5},{8,6},{9,7},{10,... | collective-permute-start | bytes 737288 | tf_op jit(solution)/shard_map/ppermute | solution.py:357
  103.7 13.0 %collective-permute-start.14 = (bf16[64,2560]{1,0:T(8,128)(2,1)S(1)}, bf16[64,2560]{1,0:T(8,128)(2,1)S(1)}, u32[]{:S(2)}, u32[]{:S(2)}) collective-permute-start(bf16[64,2560]{1,0:T(8,128)(2,1)S(1)} %collective-permute-done.12.refs_0_), channel_id=1, source_target_pairs={{0,1},{1,0},{2,3},{3,2},{4,5},{5,4},{6,7},{7,6},{8,9},{9,8},{10,11... | collective-permute-start | bytes 983048 | tf_op jit(solution)/shard_map/ppermute | solution.py:360
  106.8 9.9 %collective-permute-start.15 = (bf16[48,2560]{1,0:T(8,128)(2,1)S(1)}, bf16[48,2560]{1,0:T(8,128)(2,1)S(1)}, u32[]{:S(2)}, u32[]{:S(2)}) collective-permute-start(bf16[48,2560]{1,0:T(8,128)(2,1)S(1)} %collective-permute-done.13.refs_1_), channel_id=1, source_target_pairs={{0,1},{1,0},{2,3},{3,2},{4,5},{5,4},{6,7},{7,6},{8,9},{9,8},{10,11... | collective-permute-start | bytes 737288 | tf_op jit(solution)/shard_map/ppermute | solution.py:360
  106.8 10.8 %collective-permute-start.11 = (bf16[4,8,1792]{2,1,0:T(8,128)(2,1)S(1)}, bf16[4,8,1792]{2,1,0:T(8,128)(2,1)S(1)}, u32[]{:S(2)}, u32[]{:S(2)}) collective-permute-start(bf16[4,8,1792]{2,1,0:T(8,128)(2,1)S(1)} %get-tuple-element.58.acc_a), channel_id=1, source_target_pairs={{0,16},{32,48},{64,80},{96,112},{128,144},{160,176},{192,208},{224... | collective-permute-start | bytes 344072 | tf_op jit(solution)/shard_map/ppermute | solution.py:417
  146.9 16.0 %collective-permute-start.31 = (bf16[2,8,1792]{2,1,0:T(8,128)(2,1)S(1)}, bf16[2,8,1792]{2,1,0:T(8,128)(2,1)S(1)}, u32[]{:S(2)}, u32[]{:S(2)}) collective-permute-start(bf16[2,8,1792]{2,1,0:T(8,128)(2,1)S(1)} %get-tuple-element.79), channel_id=1, source_target_pairs={{64,32},{192,160},{65,33},{193,161},{66,34},{194,162},{67,35},{195... | collective-permute-start | bytes 172040 | tf_op jit(solution)/shard_map/ppermute | solution.py:501
  148.2 14.7 %collective-permute-start.32 = (bf16[2,8,1792]{2,1,0:T(8,128)(2,1)S(1)}, bf16[2,8,1792]{2,1,0:T(8,128)(2,1)S(1)}, u32[]{:S(2)}, u32[]{:S(2)}) collective-permute-start(bf16[2,8,1792]{2,1,0:T(8,128)(2,1)S(1)} %get-tuple-element.79), channel_id=1, source_target_pairs={{64,96},{192,224},{65,97},{193,225},{66,98},{194,226},{67,99},{195... | collective-permute-start | bytes 172040 | tf_op jit(solution)/shard_map/ppermute | solution.py:502
  (20 other events, 213.4 us)

commit v3 on v2

v3 whole, which is shorter than its diff:
```python
import functools

import jax
import jax.numpy as jnp
from jax import lax
from jax.experimental import pallas as pl
from jax.experimental.pallas import tpu as pltpu
from jax.sharding import PartitionSpec as P


BF = jnp.bfloat16
F32 = jnp.float32
PREP_LIMIT = 61
VMEM_SPEC = pl.BlockSpec(memory_space=pltpu.VMEM)
SMEM_SPEC = pl.BlockSpec(memory_space=pltpu.SMEM)


def dot(a, b, ca, cb):
    return lax.dot_general(a, b, (((ca,), (cb,)), ((), ())), preferred_element_type=F32)


def call(body, outs, live, *args, scratch=(), specs=None, limit=10):
    return pl.pallas_call(
        body,
        out_shape=outs,
        in_specs=[SMEM_SPEC] + [spec or VMEM_SPEC for spec in (specs or [None] * len(args))],
        out_specs=jax.tree.map(lambda _: VMEM_SPEC, outs),
        scratch_shapes=list(scratch),
        compiler_params=pltpu.CompilerParams(vmem_limit_bytes=limit << 20),
    )(live, *args)


def live_leaf(sc_ref):
    return sc_ref[0, 0]


def live_up(sc_ref):
    return sc_ref[0, 1]


def col_id():
    return lax.axis_index("col")


def node_level():
    leaf = lax.axis_index("leaf")
    level = jnp.where(leaf > 0, 1, 0)
    for height in range(1, lax.axis_size("leaf").bit_length() - 1):
        level = level + jnp.where((leaf > 0) & (lax.rem(leaf, 2**height) == 0), 1, 0)
    return level


def row_mask(shape, live):
    return lax.broadcasted_iota(jnp.int32, shape, 1) < live


def one_pick(wanted, j):
    lanes = lax.broadcasted_iota(jnp.int32, wanted.shape, 1) + j * 128
    return jnp.where(wanted == lanes, 1.0, 0.0).astype(BF)


def picks_kernel(map_ref, pick_ref):
    slots, _, rows = pick_ref.shape


    @pl.loop(0, slots)
    def _(s):
        wanted = map_ref[s]

        @pl.loop(0, rows // 128)
        def _(j):
            pick_ref[s, :, pl.ds(pl.multiple_of(j * 128, 128), 128)] = one_pick(wanted, j)


def make_picks(wide, rows):
    slots, tile_len, _ = wide.shape
    return pl.pallas_call(
        picks_kernel,
        out_shape=jax.ShapeDtypeStruct((slots, tile_len, rows), BF),
        in_specs=[VMEM_SPEC],
        out_specs=VMEM_SPEC,
        compiler_params=pltpu.CompilerParams(vmem_limit_bytes=10 << 20),
        name="make_picks",
    )(wide)


def leaf_up_kernel(sc_ref, parts_ref, map_ref, rows_ref, acc_ref, base_ref, z_ref):
    slots, tile_len, _ = map_ref.shape
    groups, part = parts_ref.shape[:2]
    rows = base_ref.shape[1]
    rows_dev, size = rows // (2 * groups), slots * tile_len
    total = parts_ref[0, :, :size].astype(F32)
    for k in range(1, groups):
        total = total + parts_ref[k, :, :size].astype(F32)
    for s in range(slots):
        z_ref[s] = total[:, s * tile_len : (s + 1) * tile_len]

    @pl.loop(0, slots)
    def _(s):
        z = z_ref[s].astype(BF)
        wanted = map_ref[s]

        for j in range(rows // 256):
            pick = jnp.concatenate([one_pick(wanted, 2 * j), one_pick(wanted, 2 * j + 1)], axis=1)
            acc_ref[s, :, j * 256 : (j + 1) * 256] = dot(z, pick, 1, 0).astype(BF)

    pieces = []
    for g in range(groups):
        for p in range(2):
            pieces.append(parts_ref[g, :, size + 128 * p : size + 128 * (p + 1)].astype(F32)[:, :rows_dev])
    base_ref[...] = jnp.concatenate(pieces, axis=1).astype(BF)
    high = (rows_ref[...] >> 7).astype(F32)
    low = (rows_ref[...] & 127).astype(F32)
    acc_ref[slots] = jnp.zeros((part, rows), BF)
    acc_ref[slots, :, :tile_len] = jnp.concatenate([high, low], axis=0).astype(BF)


def up_kernel(height, sc_ref, base_ref, acc_a, acc_b, y_old, inv_ref, upd_ref, pick_ref, *outs):
    y_ref = outs[0]
    mask = row_mask(base_ref.shape, live_up(sc_ref))
    left = base_ref[...].astype(F32) - (acc_a[0].astype(F32) + acc_b[0].astype(F32))
    r = jnp.where(mask, left, 0.0).astype(BF)
    half = r.shape[1] // 2
    y = jnp.concatenate(
        [dot(r[:, :half], inv_ref[:half, :half], 1, 1), dot(r, inv_ref[half:, :], 1, 1)], axis=1
    )
    y = jnp.where(mask, y, 0.0).astype(BF)
    y_ref[...] = jnp.where(node_level() == height, y, y_old[...])
    if len(outs) > 1:
        acc_ref = outs[1]


        @pl.loop(0, acc_ref.shape[0])
        def _(s):
            z = dot(y, upd_ref[s], 1, 0).astype(BF)
            moved = dot(z, pick_ref[s], 1, 0)
            acc_ref[s] = (acc_a[s + 1].astype(F32) + acc_b[s + 1].astype(F32) + moved).astype(BF)


def down_kernel(height, sc_ref, y_ref, abo_a, abo_b, x_old, inv_ref, upd_ref, pick_ref, x_ref, out_ref):
    slots = out_ref.shape[0] - 1
    mask = row_mask(y_ref.shape, live_up(sc_ref))

    def pull(s, left):
        above = abo_a[s] + abo_b[s]
        out_ref[s + 1] = above
        tile = dot(above, pick_ref[s], 1, 1).astype(BF)
        return left - dot(tile, upd_ref[s], 1, 1)

    left = lax.fori_loop(0, slots, pull, y_ref[...].astype(F32))
    v = jnp.where(mask, left, 0.0).astype(BF)
    half = v.shape[1] // 2
    x = jnp.concatenate(
        [dot(v, inv_ref[:, :half], 1, 0), dot(v[:, half:], inv_ref[half:, half:], 1, 0)], axis=1
    )
    x = jnp.where(mask, x, 0.0).astype(BF)
    out_ref[0] = x
    x_ref[...] = jnp.where(node_level() == height, x, x_old[...])


def tiles_kernel(sc_ref, above_ref, pick_ref, tile_ref):
    slots, tile_len, _ = pick_ref.shape


    @pl.loop(0, slots)
    def _(s):
        here = pl.ds(pl.multiple_of(s * tile_len, 128), tile_len)
        tile_ref[:, here] = dot(above_ref[s], pick_ref[s], 1, 1).astype(BF)


def own_tiles_kernel(sc_ref, above_ref, map_ref, tile_ref):
    slots, tile_len, _ = map_ref.shape
    rows = above_ref.shape[2]

    @pl.loop(0, slots)
    def _(s):
        here = pl.ds(pl.multiple_of(s * tile_len, 128), tile_len)
        wanted = map_ref[s]
        above = above_ref[s]
        total = jnp.zeros((above.shape[0], tile_len), F32)
        for j in range(rows // 256):
            pick = jnp.concatenate([one_pick(wanted, 2 * j), one_pick(wanted, 2 * j + 1)], axis=1)
            total = total + dot(above[:, j * 256 : (j + 1) * 256], pick, 1, 1)
        tile_ref[:, here] = total.astype(BF)


def place(col, half, upd, inv_ref, upd_ref, blocks):
    count, low = half.shape
    tiles, spare = low // 128, (inv_ref.shape[1] - low) // 128
    base = col * count
    other = (blocks - 1 - col) * count

    @pl.loop(0, count // 16)
    def _(i):
        at = pl.ds(pl.multiple_of(i * 16, 16), 16)
        here = pl.ds(pl.multiple_of(base + i * 16, 16), 16)
        there = pl.ds(pl.multiple_of(other + i * 16, 16), 16)
        for s in range(upd_ref.shape[0]):
            upd_ref[s, here, :] = upd[s, at, :]

        @pl.when(col >= tiles)
        def _():
            inv_ref[here, :low] = half[at, :]

        @pl.when(col < tiles)
        def _():
            for k in range(tiles):
                tile = half[at, k * 128 : (k + 1) * 128].astype(F32)
                own = jnp.full(tile.shape, jnp.where(col >= k, 1, 0), jnp.int32) == 1
                inv_ref[here, k * 128 : (k + 1) * 128] = jnp.where(own, tile, 0.0).astype(BF)
                m = tiles - 1 - k
                if m < spare:
                    to = low + m * 128
                    inv_ref[there, to : to + 128] = jnp.where(own, 0.0, tile).astype(BF)
            inv_ref[here, low:] = jnp.zeros((16, spare * 128), BF)


def gather_kernel(blocks, origins, sc_ref, *refs):
    count = len(origins)
    halves, upds, (inv_ref, upd_ref) = refs[:count], refs[count : 2 * count], refs[-2:]
    for half, upd, (shift, flip) in zip(halves, upds, origins):
        col = lax.rem(col_id() + 2 * shift + blocks, blocks)
        if flip:
            col = col + 1 - 2 * lax.rem(col, 2)
        place(col, half, upd, inv_ref, upd_ref, blocks)


def live_kernel(sc_ref, r_ref, out_ref):
    alive = lax.broadcasted_iota(jnp.int32, r_ref.shape, 0) < live_leaf(sc_ref)
    out_ref[...] = jnp.where(alive, r_ref[...].astype(F32), 0.0).astype(BF)


def prep_kernel(
    sc_ref,
    r_ref,
    fold_ref,
    sides_hbm,
    up_inv_hbm,
    inv_hbm,
    upd_hbm,
    half_ref,
    y_ref,
    keep_ref,
    send_ref,
    base_ref,
    up_inv_ref,
    inv_ref,
    upd_ref,
    sems,
):
    moves = [
        pltpu.make_async_copy(src, dst, sems.at[k])
        for k, (src, dst) in enumerate(
            (
                (up_inv_hbm.at[0], up_inv_ref),
                (inv_hbm.at[0], inv_ref),
                (upd_hbm.at[0], upd_ref),
                (sides_hbm.at[0, 1], base_ref),
            )
        )
    ]
    for move in moves:
        move.start()
    moves[0].wait()
    col = col_id()
    low = half_ref.shape[1]
    tiles, spare = low // 128, fold_ref.shape[1] // 128
    for k in range(tiles):
        mine = up_inv_ref[:, k * 128 : (k + 1) * 128]
        m = tiles - 1 - k
        if m < spare:
            other = fold_ref[:, m * 128 : (m + 1) * 128]
        else:
            other = jnp.zeros_like(mine)
        own = jnp.where((col >= tiles) | (col >= k), 1, 0)
        keep = jnp.full(mine.shape, own, jnp.int32) == 1
        tile = jnp.where(keep, mine.astype(F32), other.astype(F32)).astype(BF)
        half_ref[:, k * 128 : (k + 1) * 128] = tile
    rows_dev = inv_ref.shape[0]
    groups, part, _ = keep_ref.shape
    mask = lax.broadcasted_iota(jnp.int32, y_ref.shape, 0) + col * rows_dev < live_leaf(sc_ref)
    moves[1].wait()
    y = jnp.where(mask, dot(inv_ref[...], r_ref[...], 1, 0), 0.0)
    y_ref[...] = y.astype(BF)
    turned = y.T.astype(BF)
    core = lax.rem(col, 2)
    slots, size = upd_ref.shape[0], upd_ref.shape[2]
    first = jnp.full((part, size), core, jnp.int32) == 0
    moves[2].wait()
    for s in range(slots):
        term = dot(turned, upd_ref[s], 1, 0)
        for g in range(groups):
            a = term[2 * g * part : (2 * g + 1) * part]
            b = term[(2 * g + 1) * part : (2 * g + 2) * part]
            keep_ref[g, :, s * size : (s + 1) * size] = jnp.where(first, a, b).astype(BF)
            send_ref[g, :, s * size : (s + 1) * size] = jnp.where(first, b, a).astype(BF)
    moves[3].wait()
    base = base_ref[...].astype(F32)
    base = jnp.concatenate([base, jnp.zeros((128 - rows_dev, base.shape[1]), F32)], axis=0).T
    first = jnp.full((part, 128), core, jnp.int32) == 0
    for g in range(groups):
        a = base[2 * g * part : (2 * g + 1) * part]
        b = base[(2 * g + 1) * part : (2 * g + 2) * part]
        keep_ref[g, :, slots * size :] = jnp.where(first, a, b).astype(BF)
        send_ref[g, :, slots * size :] = jnp.where(first, b, a).astype(BF)


def join_terms_kernel(sc_ref, keep_ref, got_ref, out_ref):
    groups, part, wide = keep_ref.shape
    size = wide - 128
    first = jnp.full((part, 128), lax.rem(col_id(), 2), jnp.int32) == 0
    for g in range(groups):
        both = keep_ref[g, :, :size].astype(F32) + got_ref[g, :, :size].astype(F32)
        out_ref[g, :, :size] = both.astype(BF)
        own, other = keep_ref[g, :, size:].astype(F32), got_ref[g, :, size:].astype(F32)
        out_ref[g, :, size : size + 128] = jnp.where(first, own, other).astype(BF)
        out_ref[g, :, size + 128 :] = jnp.where(first, other, own).astype(BF)


def leaf_bwd_kernel(sc_ref, tile_ref, y_ref, upd_ref, inv_ref, x_ref, keep_ref, send_ref):
    rows_dev, width = y_ref.shape
    groups, part = keep_ref.shape[0], x_ref.shape[0]
    slots, size = upd_ref.shape[0], upd_ref.shape[2]
    left = y_ref[...].astype(F32)
    for s in range(slots):
        left = left - dot(upd_ref[s], tile_ref[:, s * size : (s + 1) * size], 1, 1)
    mask = lax.broadcasted_iota(jnp.int32, left.shape, 0) + col_id() * rows_dev < live_leaf(sc_ref)
    v = jnp.where(mask, left, 0.0).astype(BF)
    term = dot(inv_ref[...], v, 0, 0)
    core = lax.rem(col_id(), 2)
    first = jnp.full((rows_dev, width), core, jnp.int32) == 0
    first_x = jnp.full((16, 128), core, jnp.int32) == 0
    x = x_ref[...].astype(F32)

    def block(at):
        piece = x[:, at * rows_dev : (at + 1) * rows_dev]
        piece = jnp.concatenate([piece, jnp.zeros((part, 128 - rows_dev), F32)], axis=1)
        return jnp.concatenate([piece, jnp.zeros((16 - part, 128), F32)], axis=0)

    for g in range(groups):
        a = term[2 * g * rows_dev : (2 * g + 1) * rows_dev]
        b = term[(2 * g + 1) * rows_dev : (2 * g + 2) * rows_dev]
        keep_ref[g, :rows_dev] = jnp.where(first, a, b).astype(BF)
        send_ref[g, :rows_dev] = jnp.where(first, b, a).astype(BF)
        xa, xb = block(2 * g), block(2 * g + 1)
        keep_ref[g, rows_dev:] = jnp.where(first_x, xa, xb).astype(BF)
        send_ref[g, rows_dev:] = jnp.where(first_x, xb, xa).astype(BF)


def merge_kernel(sc_ref, keep_ref, got_ref, out_ref):
    rows_dev = keep_ref.shape[1] - 16
    first = jnp.full((16, 128), lax.rem(col_id(), 2), jnp.int32) == 0
    for g in range(keep_ref.shape[0]):
        both = keep_ref[g, :rows_dev].astype(F32) + got_ref[g, :rows_dev].astype(F32)
        out_ref[g, :rows_dev] = both.astype(BF)
        own, other = keep_ref[g, rows_dev:].astype(F32), got_ref[g, rows_dev:].astype(F32)
        out_ref[g, rows_dev : rows_dev + 16] = jnp.where(first, own, other).astype(BF)
        out_ref[g, rows_dev + 16 :] = jnp.where(first, other, own).astype(BF)


def final_kernel(sc_ref, in_ref, out_ref, wide_ref):
    rows_dev = out_ref.shape[1]
    groups, part = in_ref.shape[0], out_ref.shape[2] // (2 * in_ref.shape[0])
    total = in_ref[0, :rows_dev].astype(F32)
    for g in range(1, groups):
        total = total + in_ref[g, :rows_dev].astype(F32)
    mask = lax.broadcasted_iota(jnp.int32, total.shape, 0) + col_id() * rows_dev < live_leaf(sc_ref)
    out_ref[0] = jnp.where(mask, total, 0.0).astype(BF)
    for g in range(groups):
        for p in range(2):
            at, to = rows_dev + 16 * p, (2 * g + p) * part
            wide_ref[to : to + part] = in_ref[g, at : at + 16].astype(F32)[:part]
    out_ref[1] = wide_ref[...].T[:rows_dev].astype(BF)


def shards(
    right_sides, leaf_inverse, upper_inverse, leaf_update, upper_update, live_rows, tile_map
):
    leaf_count = lax.axis_size("leaf")
    col_count = lax.axis_size("col")
    depth = leaf_count.bit_length() - 1
    rows_dev = leaf_inverse.shape[1]
    rows = leaf_inverse.shape[2]
    width = right_sides.shape[3]
    part = width // col_count
    tile_len = tile_map.shape[3]
    leaf_id = lax.axis_index("leaf")

    live_rows = jnp.minimum(live_rows, leaf_inverse.shape[2])
    wide_map = jnp.broadcast_to(tile_map[0, :, :, :, None], (2, depth, tile_len, 128))
    shape = jax.ShapeDtypeStruct
    blocks = col_count
    groups = blocks // 2
    low = rows // 2 + 128
    pairs = [(i, i ^ 1) for i in range(blocks)]
    members = [list(range(p, blocks, 2)) for p in range(2)]

    def along(x, step):
        return lax.ppermute(x, "col", [(i, (i + 2 * step) % blocks) for i in range(blocks)])

    def partner(x):
        return lax.ppermute(x, "col", pairs)

    fold = lax.ppermute(
        upper_inverse[0, :, low:],
        "col",
        [(i, blocks - 1 - i) for i in range(blocks // 2, blocks)],
    )
    r_leaf = lax.all_gather(right_sides[0, 0], "col", axis=0, tiled=True)
    r_leaf = call(live_kernel, shape(r_leaf.shape, BF), live_rows, r_leaf)
    fold, r_leaf = lax.optimization_barrier((fold, r_leaf))
    hbm = pl.BlockSpec(memory_space=pltpu.HBM)
    half, y_leaf, keep, send = call(
        prep_kernel,
        [shape((rows_dev, low), BF), shape((rows_dev, width), BF)]
        + [shape((groups, part, depth * tile_len + 128), BF)] * 2,
        live_rows,
        r_leaf,
        fold,
        right_sides,
        upper_inverse,
        leaf_inverse,
        leaf_update,
        limit=PREP_LIMIT,
        specs=[None, None] + [hbm] * 4,
        scratch=[
            pltpu.VMEM((rows_dev, width), BF),
            pltpu.VMEM((rows_dev, rows), BF),
            pltpu.VMEM((rows_dev, rows), BF),
            pltpu.VMEM((depth, rows_dev, tile_len), BF),
            pltpu.SemaphoreType.DMA((4,)),
        ],
    )
    got = partner(send)
    terms = call(
        join_terms_kernel, shape((groups, part, depth * tile_len + 256), BF), live_rows, keep, got
    )
    swapped = lax.all_to_all(terms, "col", 0, 0, axis_index_groups=members)
    own_upd = upper_update[0, : depth - 1]
    half_a = half_b = half
    upd_a = upd_b = own_upd
    halves, upds, origins = [half, partner(half)], [own_upd, partner(own_upd)], [(0, 0), (0, 1)]
    far = groups // 2
    for hop in range(1, far):
        upd_a, upd_b = along(upd_a, 1), along(upd_b, -1)
        half_a, half_b = along(half_a, 1), along(half_b, -1)
        halves += [half_a, half_b, partner(half_a), partner(half_b)]
        upds += [upd_a, upd_b, partner(upd_a), partner(upd_b)]
        origins += [(-hop, 0), (hop, 0), (-hop, 1), (hop, 1)]
    upd_far = along(upd_b, -1)
    half_far = along(half_a, 1)
    last = [half_far, partner(half_far), upd_far, partner(upd_far)]
    last_origins = [(far, 0), (far, 1)]
    acc, base_up = call(
        leaf_up_kernel,
        [shape((depth + 1, part, rows), BF), shape((part, rows), BF)],
        live_rows,
        swapped,
        wide_map[0],
        tile_map[0, 0],
        scratch=[pltpu.VMEM((depth, part, tile_len), F32)],
    )
    from_leaf = lax.ppermute(acc, "leaf", [(i, i + 1) for i in range(0, leaf_count, 2)])
    pick_up = make_picks(wide_map[1, : depth - 1], rows)
    gathered = [shape((rows, rows), BF), shape((depth - 1, rows, tile_len), BF)]
    inv_up, upd_up = call(
        functools.partial(gather_kernel, blocks, origins), gathered, live_rows, *halves, *upds
    )
    inv_up, upd_up = pl.pallas_call(
        functools.partial(gather_kernel, blocks, last_origins),
        out_shape=gathered,
        in_specs=[SMEM_SPEC] + [VMEM_SPEC] * 6,
        out_specs=[VMEM_SPEC] * 2,
        input_output_aliases={5: 0, 6: 1},
        compiler_params=pltpu.CompilerParams(vmem_limit_bytes=10 << 20),
        name="gather_far",
    )(live_rows, *last, inv_up, upd_up)


    nodes = range(1, leaf_count)

    def level_of(node):
        return (node & -node).bit_length()

    y_up = jnp.zeros((part, rows), BF)
    for height in range(1, depth + 1):
        if height == 1:
            acc_a = acc
            acc_b = from_leaf
        else:
            step = 2 ** (height - 2)
            ups = [i for i in nodes if level_of(i) == height]
            acc_a = lax.ppermute(acc, "leaf", [(i - step, i) for i in ups])
            acc_b = lax.ppermute(acc, "leaf", [(i + step, i) for i in ups])
        if height == 2:
            acc_a, acc_b, next_pick = lax.optimization_barrier((acc_a, acc_b, next_pick))
        outs = [shape((part, rows), BF)]
        if height < depth:
            outs.append(shape((depth - height, part, rows), BF))
        y_up, *rest = call(
            functools.partial(up_kernel, height),
            outs,
            live_rows,
            base_up,
            acc_a,
            acc_b,
            y_up,
            inv_up,
            upd_up,
            pick_up,
        )
        if rest:
            acc = rest[0]
        if height == 1:
            acc, carried = lax.optimization_barrier((acc, from_leaf[depth, :, :tile_len]))
            carried = carried.astype(F32)
            next_map = (carried[:depth] * 128 + carried[depth:]).astype(jnp.int32)
            wide_next = jnp.broadcast_to(next_map[:, :, None], (depth, tile_len, 128))
            next_pick = make_picks(wide_next, rows)

    x_up = jnp.zeros((part, rows), BF)
    abo_a = abo_b = jnp.zeros((1, part, rows), BF)
    for height in range(depth, 0, -1):
        x_up, above = call(
            functools.partial(down_kernel, height),
            [shape((part, rows), BF), shape((depth - height + 1, part, rows), BF)],
            live_rows,
            y_up,
            abo_a,
            abo_b,
            x_up,
            inv_up,
            upd_up,
            pick_up,
        )
        if height == 1:
            sent = call(
                tiles_kernel, shape((part, depth * tile_len), BF), live_rows, above, next_pick
            )
            got = lax.ppermute(sent, "leaf", [(i + 1, i) for i in range(0, leaf_count, 2)])
        else:
            step = 2 ** (height - 2)
            ups = [i for i in nodes if level_of(i) == height]
            abo_a = lax.ppermute(above, "leaf", [(i, i - step) for i in ups])
            abo_b = lax.ppermute(above, "leaf", [(i, i + step) for i in ups])

    tiles = call(
        own_tiles_kernel, shape((part, depth * tile_len), BF), live_rows, above, wide_map[0]
    )
    tiles = jnp.where(leaf_id % 2 == 1, tiles, got)
    tiles = lax.all_gather(tiles, "col", axis=0, tiled=True)
    keep, send = call(
        leaf_bwd_kernel,
        [shape((groups, rows_dev + 16, width), BF)] * 2,
        live_rows,
        tiles,
        y_leaf,
        leaf_update[0],
        leaf_inverse[0],
        x_up,
    )
    merged = call(
        merge_kernel, shape((groups, rows_dev + 32, width), BF), live_rows, keep, partner(send)
    )
    swapped = lax.all_to_all(merged, "col", 0, 0, axis_index_groups=members)
    return call(
        final_kernel,
        shape((2, rows_dev, width), BF),
        live_rows,
        swapped,
        scratch=[pltpu.VMEM((width, 128), F32)],
    )[None]


def solution(mesh):
    placed = (
        P("leaf", None, "col", None),
        P("leaf", "col", None),
        P("leaf", "col", None),
        P("leaf", None, "col", None),
        P("leaf", None, "col", None),
        P("leaf", None),
        P("leaf", None, None, None),
    )

    return jax.shard_map(
        shards, mesh=mesh, in_specs=placed, out_specs=P("leaf", None, "col", None), check_vma=False
    )
```

time: 225 us -> 216 us (0.960)
  waiting for transfers between devices: 61.2 us -> 41.8 us
  blocking collectives: 53 us -> 58.9 us
  local copies, waits for them, and re-layouts: 10 us -> 14.7 us
  starting transfers between devices: 50.5 us -> 48.2 us
    ppermute x10 -> x14, waiting for transfers between devices: 33.9 us -> 13.5 us  [along(): lax.ppermute(x, 'col', [(i, (i + 2 * step) % blocks) for i in range(block...]
    unnamed x12 -> x60, local copies, waits for them, and re-layouts: 3.02 us -> 10.3 us
    all_gather x1, blocking collectives: 19.2 us -> 24.2 us  [shards(): r_leaf = lax.all_gather(right_sides[0, 0], 'col', axis=0, tiled=True)]
    all_to_all x1, starting transfers between devices: 7.43 us -> 4.3 us  [shards(): swapped = lax.all_to_all(terms, 'col', 0, 0, axis_index_groups=members)]
    ppermute x1 -> x0, starting transfers between devices: 3.09 us -> none  [shards(): lax.ppermute(tile_map[0, 0], 'leaf', [(i, i + 1) for i in range(0, leaf_c...]
    ppermute x10 -> x14, starting transfers between devices: 20.5 us -> 22.2 us  [along(): lax.ppermute(x, 'col', [(i, (i + 2 * step) % blocks) for i in range(block...]
    pallas_call x20 -> x19, Pallas kernels: 45.3 us -> 46.1 us  [the longest x18 44.7 us: call(): pl.pallas_call(body, out_shape=outs, in_specs=[SMEM_SPEC] + [spec or VMEM...]
  transfers between devices with their start and end apart: 38 -> 48, of which waited for: 17 -> 16; matrix products, arithmetic and copies ran while one was open for 3% -> 2% of each run, Pallas kernels for 8% -> 9%
where the time goes in v3:
time: 216 us; the launch traced here: 214 us
  blocking collectives  58.9 us (27%)
  Pallas kernels  49.3 us (23%)
  starting transfers between devices  48.2 us (22%)
  waiting for transfers between devices  41.8 us (19%)
  local copies, waits for them, and re-layouts  14.7 us (7%)
    pallas_call x18, Pallas kernels, call(): pl.pallas_call(body, out_shape=outs, in_specs=[SMEM_SPEC] + [spec or VMEM...  44.7 us
    all_gather x1, blocking collectives, shards(): r_leaf = lax.all_gather(right_sides[0, 0], 'col', axis=0, tiled=True)  24.2 us
    ppermute x14, starting transfers between devices, along(): lax.ppermute(x, 'col', [(i, (i + 2 * step) % blocks) for i in range(block...  22.2 us
    all_to_all x1, blocking collectives, shards(): swapped = lax.all_to_all(merged, 'col', 0, 0, axis_index_groups=members)  18.8 us
    all_gather x1, blocking collectives, shards(): tiles = lax.all_gather(tiles, 'col', axis=0, tiled=True)  15.8 us
    ppermute x3, waiting for transfers between devices, shards(): abo_a = lax.ppermute(above, 'leaf', [(i, i - step) for i in ups])  14.8 us
    ppermute x14, waiting for transfers between devices, along(): lax.ppermute(x, 'col', [(i, (i + 2 * step) % blocks) for i in range(block...  13.5 us
    unnamed x60, local copies, waits for them, and re-layouts  10.3 us
  transfers between devices with their start and end apart: 48, of which 16 were waited for; matrix products, arithmetic and copies ran while one was open for 2% of the time, Pallas kernels for 9%

profile of v3, /device:TPU:4, one launch (start us, length us, event | category | flops | bytes accessed | tf_op | source)
XLA Modules:
  0.0 214.1 jit_solution(1251327791387650989)
XLA Ops:
  1.0 5.9 %collective-permute-start.8 = (bf16[3,112,512]{2,1,0:T(8,128)(2,1)S(1)}, bf16[3,112,512]{2,1,0:T(8,128)(2,1)S(1)}, u32[]{:S(2)}, u32[]{:S(2)}) collective-permute-start(bf16[3,112,512]{2,1,0:T(8,128)(2,1)S(1)} %slice_bitcast_fusion.refs_14_), channel_id=1, source_target_pairs={{0,14},{1,15},{2,0},{3,1},{4,2},{5,3},{6,4},{7,5},{8,6},{9,7},{10,... | collective-permute-start | bytes 1032200 | tf_op jit(solution)/shard_map/ppermute | solution.py:399
  10.6 24.2 %all-gather = bf16[1,1,1792,128]{3,2,1,0:T(8,128)(2,1)S(1)} all-gather(bf16[1,1,112,128]{3,2,1,0:T(8,128)(2,1)S(1)} %slice.30), channel_id=2, replica_groups=mesh['leaf'=16,'col'=16] {'col'}, dimensions={2}, use_global_device_ids=true | all-gather | bytes 487424 | tf_op jit(solution)/shard_map/all_gather | solution.py:409
  37.0 3.7 %shard_map.74 = (bf16[112,1024]{1,0:T(8,128)(2,1)}, bf16[112,128]{1,0:T(8,128)(2,1)}, bf16[8,8,2176]{2,1,0:T(8,128)(2,1)}, bf16[8,8,2176]{2,1,0:T(8,128)(2,1)}) custom-call(s32[1,2]{1,0:T(1,128)} %copy-done.23, bf16[1792,128]{1,0:T(8,128)(2,1)} %copy-done, bf16[112,768]{1,0:T(8,128)(2,1)} %copy-done.28, bf16[1,2,112,128]{3,2,1,0:T(8,128)(2,1)} %sides_hbm.1, ...), custom_call_target="tpu_custom_call" | custom-call | tf_op jit(solution)/shard_map/pallas_call | solution.py:23
  40.7 2.9 %collective-permute-start.3 = (bf16[112,1024]{1,0:T(8,128)(2,1)}, bf16[112,1024]{1,0:T(8,128)(2,1)S(1)}, u32[]{:S(2)}, u32[]{:S(2)}) collective-permute-start(bf16[112,1024]{1,0:T(8,128)(2,1)} %get-tuple-element.44.refs_0_), channel_id=1, source_target_pairs={{0,2},{1,3},{2,4},{3,5},{4,6},{5,7},{6,8},{7,9},{8,10},{9,11},{10,... | collective-permute-start | bytes 688136 | tf_op jit(solution)/shard_map/ppermute | solution.py:399
  44.6 5.4 %collective-permute-done.3.refs_2_ = bf16[112,1024]{1,0:T(8,128)(2,1)S(1)} collective-permute-done((bf16[112,1024]{1,0:T(8,128)(2,1)}, bf16[112,1024]{1,0:T(8,128)(2,1)S(1)}, u32[]{:S(2)}, u32[]{:S(2)}) %collective-permute-start.3) | collective-permute-done | bytes 229408 | tf_op jit(solution)/shard_map/ppermute | solution.py:399
  56.0 2.1 collective-permute-done.4.refs_6_
  61.7 4.0 %collective-permute-done.9.refs_21_ = bf16[3,112,512]{2,1,0:T(8,128)(2,1)S(1)} collective-permute-done((bf16[3,112,512]{2,1,0:T(8,128)(2,1)S(1)}, bf16[3,112,512]{2,1,0:T(8,128)(2,1)S(1)}, u32[]{:S(2)}, u32[]{:S(2)}) %collective-permute-start.9) | collective-permute-done | bytes 344096 | tf_op jit(solution)/shard_map/ppermute | solution.py:399
  65.8 2.6 %collective-permute-start.20 = (bf16[112,1024]{1,0:T(8,128)(2,1)}, bf16[112,1024]{1,0:T(8,128)(2,1)}, u32[]{:S(2)}, u32[]{:S(2)}) collective-permute-start(bf16[112,1024]{1,0:T(8,128)(2,1)} %collective-permute-done.17.refs_7_), channel_id=1, source_target_pairs={{0,14},{1,15},{2,0},{3,1},{4,2},{5,3},{6,4},{7,5},{8,6},{9,7},{10,... | collective-permute-start | bytes 688136 | tf_op jit(solution)/shard_map/ppermute | solution.py:399
  70.6 2.0 collective-permute-start.30
  75.6 4.3 %all-to-all-start = ((bf16[8,8,2304]{2,1,0:T(8,128)(2,1)}), bf16[8,8,2304]{2,1,0:T(8,128)(2,1)S(1)}, u32[]{:S(2)}, u32[]{:S(2)}) async-start(bf16[8,8,2304]{2,1,0:T(8,128)(2,1)} %shard_map.75), calls=%async_computation | async-start | bytes 589824 | tf_op jit(solution)/shard_map/all_to_all | solution.py:438
  88.3 2.6 %all-to-all-done.parts_ref = bf16[8,8,2304]{2,1,0:T(8,128)(2,1)S(1)} async-done(((bf16[8,8,2304]{2,1,0:T(8,128)(2,1)}), bf16[8,8,2304]{2,1,0:T(8,128)(2,1)S(1)}, u32[]{:S(2)}, u32[]{:S(2)}) %all-to-all-start) | async-done | bytes 294944 | tf_op jit(solution)/shard_map/all_to_all | solution.py:438
  94.2 3.2 %collective-permute-start.2 = (bf16[5,8,1792]{2,1,0:T(8,128)(2,1)S(1)}, bf16[5,8,1792]{2,1,0:T(8,128)(2,1)S(1)}, u32[]{:S(2)}, u32[]{:S(2)}) collective-permute-start(bf16[5,8,1792]{2,1,0:T(8,128)(2,1)S(1)} %get-tuple-element.43.acc_a), channel_id=1, source_target_pairs={{0,16},{32,48},{64,80},{96,112},{128,144},{160,176},{192,208},{224... | collective-permute-start | bytes 430088 | tf_op jit(solution)/shard_map/ppermute | solution.py:463
  102.2 4.5 %shard_map.77 = (bf16[1792,1792]{1,0:T(8,128)(2,1)S(1)}, bf16[3,1792,512]{2,1,0:T(8,128)(2,1)S(1)}) custom-call(s32[1,2]{1,0:T(1,128)S(1)} %copy-done.25, bf16[112,1024]{1,0:T(8,128)(2,1)S(1)} %copy-done.8, bf16[112,1024]{1,0:T(8,128)(2,1)S(1)} %copy-done.14, bf16[112,1024]{1,0:T(8,128)(2,1)S(1)} %copy-done.10, bf16[112,1024]{1,0:T(8,128)(2,1)S(1)} %copy-done.12, ...), custom_call_target="tpu_custom_call" | custom-call | tf_op jit(solution)/shard_map/pallas_call | solution.py:23
  108.2 3.9 %shard_map.78 = (bf16[8,1792]{1,0:T(8,128)(2,1)S(1)}, bf16[3,8,1792]{2,1,0:T(8,128)(2,1)S(1)}) custom-call(s32[1,2]{1,0:T(1,128)S(1)} %copy-done.25, bf16[8,1792]{1,0:T(8,128)(2,1)S(1)} %get-tuple-element.42.base_ref, bf16[5,8,1792]{2,1,0:T(8,128)(2,1)S(1)} %get-tuple-element.43.acc_a, bf16[5,8,1792]{2,1,0:T(8,128)(2,1)S(1)} %collective-permute-done.2.acc_b, ...), custom_call_target="tpu_custom_call" | custom-call | tf_op jit(solution)/shard_map/pallas_call | solution.py:23
  119.8 3.3 %shard_map.79 = (bf16[8,1792]{1,0:T(8,128)(2,1)S(1)}, bf16[2,8,1792]{2,1,0:T(8,128)(2,1)S(1)}) custom-call(s32[1,2]{1,0:T(1,128)S(1)} %copy-done.25, bf16[8,1792]{1,0:T(8,128)(2,1)S(1)} %get-tuple-element.42.base_ref, bf16[3,8,1792]{2,1,0:T(8,128)(2,1)S(1)} %collective-permute-done.33.acc_a, bf16[3,8,1792]{2,1,0:T(8,128)(2,1)S(1)} %collective-permute-done.34.acc_b, ...), custom_call_target="tpu_custom_call" | custom-call | tf_op jit(solution)/shard_map/pallas_call | solution.py:23
  126.2 2.6 %shard_map.80 = (bf16[8,1792]{1,0:T(8,128)(2,1)S(1)}, bf16[1,8,1792]{2,1,0:T(8,128)(2,1)S(1)}) custom-call(s32[1,2]{1,0:T(1,128)S(1)} %copy-done.25, bf16[8,1792]{1,0:T(8,128)(2,1)S(1)} %get-tuple-element.42.base_ref, bf16[2,8,1792]{2,1,0:T(8,128)(2,1)S(1)} %collective-permute-done.35.acc_a, bf16[2,8,1792]{2,1,0:T(8,128)(2,1)S(1)} %collective-permute-done.36.acc_b, ...), custom_call_target="tpu_custom_call" | custom-call | tf_op jit(solution)/shard_map/pallas_call | solution.py:23
  134.7 2.3 %shard_map.83 = (bf16[8,1792]{1,0:T(8,128)(2,1)S(1)}, bf16[2,8,1792]{2,1,0:T(8,128)(2,1)S(1)}) custom-call(s32[1,2]{1,0:T(1,128)S(1)} %copy-done.25, bf16[8,1792]{1,0:T(8,128)(2,1)S(1)} %shard_map.81.y_ref, bf16[1,8,1792]{2,1,0:T(8,128)(2,1)S(1)} %collective-permute-done.39.abo_a, bf16[1,8,1792]{2,1,0:T(8,128)(2,1)S(1)} %collective-permute-done.40.abo_b, ...), custom_call_target="tpu_custom_call" | custom-call | tf_op jit(solution)/shard_map/pallas_call | solution.py:23
  139.0 14.0 %collective-permute-done.41.abo_a = bf16[2,8,1792]{2,1,0:T(8,128)(2,1)S(1)} collective-permute-done((bf16[2,8,1792]{2,1,0:T(8,128)(2,1)S(1)}, bf16[2,8,1792]{2,1,0:T(8,128)(2,1)S(1)}, u32[]{:S(2)}, u32[]{:S(2)}) %collective-permute-start.41) | collective-permute-done | bytes 57376 | tf_op jit(solution)/shard_map/ppermute | solution.py:544
  153.0 3.7 %shard_map.84 = (bf16[8,1792]{1,0:T(8,128)(2,1)S(1)}, bf16[3,8,1792]{2,1,0:T(8,128)(2,1)S(1)}) custom-call(s32[1,2]{1,0:T(1,128)S(1)} %copy-done.25, bf16[8,1792]{1,0:T(8,128)(2,1)S(1)} %shard_map.81.y_ref, bf16[2,8,1792]{2,1,0:T(8,128)(2,1)S(1)} %collective-permute-done.41.abo_a, bf16[2,8,1792]{2,1,0:T(8,128)(2,1)S(1)} %collective-permute-done.42.abo_b, ...), custom_call_target="tpu_custom_call" | custom-call | tf_op jit(solution)/shard_map/pallas_call | solution.py:23
  161.3 4.8 %shard_map.85 = (bf16[8,1792]{1,0:T(8,128)(2,1)S(1)}, bf16[4,8,1792]{2,1,0:T(8,128)(2,1)S(1)}) custom-call(s32[1,2]{1,0:T(1,128)S(1)} %copy-done.25, bf16[8,1792]{1,0:T(8,128)(2,1)S(1)} %shard_map.81.y_ref, bf16[3,8,1792]{2,1,0:T(8,128)(2,1)S(1)} %collective-permute-done.43.abo_a, bf16[3,8,1792]{2,1,0:T(8,128)(2,1)S(1)} %collective-permute-done.44.abo_b, ...), custom_call_target="tpu_custom_call" | custom-call | tf_op jit(solution)/shard_map/pallas_call | solution.py:23
  166.2 2.9 %shard_map.87 = bf16[8,2048]{1,0:T(8,128)(2,1)S(1)} custom-call(s32[1,2]{1,0:T(1,128)S(1)} %copy-done.26, bf16[4,8,1792]{2,1,0:T(8,128)(2,1)S(1)} %get-tuple-element.65.above_ref, bf16[4,512,1792]{2,1,0:T(8,128)(2,1)S(1)} %make_picks.3.pick_ref), custom_call_target="tpu_custom_call" | custom-call | tf_op jit(solution)/shard_map/pallas_call | solution.py:23
  170.4 2.9 %shard_map.86 = bf16[8,2048]{1,0:T(8,128)(2,1)S(1)} custom-call(s32[1,2]{1,0:T(1,128)S(1)} %copy-done.26, bf16[4,8,1792]{2,1,0:T(8,128)(2,1)S(1)} %get-tuple-element.65.above_ref, s32[4,512,128]{2,1,0:T(8,128)S(1)} %broadcast_in_dim.26.map_ref), custom_call_target="tpu_custom_call" | custom-call | tf_op jit(solution)/shard_map/pallas_call | solution.py:23
  174.9 15.8 %all_gather.7.tile_ref = bf16[128,2048]{1,0:T(8,128)(2,1)S(1)} all-gather(bf16[8,2048]{1,0:T(8,128)(2,1)S(1)} %broadcast_select_fusion), channel_id=1, replica_groups=mesh['leaf'=16,'col'=16] {'col'}, dimensions={0}, use_global_device_ids=true | all-gather | bytes 557056 | tf_op jit(solution)/shard_map/all_gather | solution.py:551
  194.0 18.8 %all_to_all.10.in_ref = bf16[8,144,128]{2,1,0:T(8,128)(2,1)S(1)} all-to-all(bf16[8,144,128]{2,1,0:T(8,128)(2,1)S(1)} %shard_map.89), channel_id=1, replica_groups={{0,2,4,6,8,10,12,14},{1,3,5,7,9,11,13,15},{16,18,20,22,24,26,28,30},{17..., dimensions={0} | all-to-all | bytes 589824 | tf_op jit(solution)/shard_map/all_to_all | solution.py:565
  (171 shorter events, 71.2 us)
Async XLA Ops:
  1.0 43.0 %collective-permute-start.8 = (bf16[3,112,512]{2,1,0:T(8,128)(2,1)S(1)}, bf16[3,112,512]{2,1,0:T(8,128)(2,1)S(1)}, u32[]{:S(2)}, u32[]{:S(2)}) collective-permute-start(bf16[3,112,512]{2,1,0:T(8,128)(2,1)S(1)} %slice_bitcast_fusion.refs_14_), channel_id=1, source_target_pairs={{0,14},{1,15},{2,0},{3,1},{4,2},{5,3},{6,4},{7,5},{8,6},{9,7},{10,... | collective-permute-start | bytes 1032200 | tf_op jit(solution)/shard_map/ppermute | solution.py:399
  7.0 37.1 %collective-permute-start.24 = (bf16[3,112,512]{2,1,0:T(8,128)(2,1)S(1)}, bf16[3,112,512]{2,1,0:T(8,128)(2,1)S(1)}, u32[]{:S(2)}, u32[]{:S(2)}) collective-permute-start(bf16[3,112,512]{2,1,0:T(8,128)(2,1)S(1)} %slice_bitcast_fusion.refs_14_), channel_id=1, source_target_pairs={{0,2},{1,3},{2,4},{3,5},{4,6},{5,7},{6,8},{7,9},{8,10},{9,11},{10,... | collective-permute-start | bytes 1032200 | tf_op jit(solution)/shard_map/ppermute | solution.py:399
  7.0 46.2 %collective-permute-start.23 = (bf16[3,112,512]{2,1,0:T(8,128)(2,1)S(1)}, bf16[3,112,512]{2,1,0:T(8,128)(2,1)S(1)}, u32[]{:S(2)}, u32[]{:S(2)}) collective-permute-start(bf16[3,112,512]{2,1,0:T(8,128)(2,1)S(1)} %slice_bitcast_fusion.refs_14_), channel_id=1, source_target_pairs={{0,1},{1,0},{2,3},{3,2},{4,5},{5,4},{6,7},{7,6},{8,9},{9,8},{10,11... | collective-permute-start | bytes 1032200 | tf_op jit(solution)/shard_map/ppermute | solution.py:402
  7.9 28.4 %collective-permute-start = (bf16[112,768]{1,0:T(8,128)(2,1)S(1)}, bf16[112,768]{1,0:T(8,128)(2,1)S(1)}, u32[]{:S(2)}, u32[]{:S(2)}) collective-permute-start(bf16[112,768]{1,0:T(8,128)(2,1)S(1)} %slice_bitcast_fusion.1), channel_id=1, source_target_pairs={{8,7},{9,6},{10,5},{11,4},{12,3},{13,2},{14,1},{15,0},{24,23},{25,... | collective-permute-start | bytes 516104 | tf_op jit(solution)/shard_map/ppermute | solution.py:404
  40.7 9.2 %collective-permute-start.3 = (bf16[112,1024]{1,0:T(8,128)(2,1)}, bf16[112,1024]{1,0:T(8,128)(2,1)S(1)}, u32[]{:S(2)}, u32[]{:S(2)}) collective-permute-start(bf16[112,1024]{1,0:T(8,128)(2,1)} %get-tuple-element.44.refs_0_), channel_id=1, source_target_pairs={{0,2},{1,3},{2,4},{3,5},{4,6},{5,7},{6,8},{7,9},{8,10},{9,11},{10,... | collective-permute-start | bytes 688136 | tf_op jit(solution)/shard_map/ppermute | solution.py:399
  44.1 11.1 %collective-permute-start.1 = (bf16[8,8,2176]{2,1,0:T(8,128)(2,1)}, bf16[8,8,2176]{2,1,0:T(8,128)(2,1)S(1)}, u32[]{:S(2)}, u32[]{:S(2)}) collective-permute-start(bf16[8,8,2176]{2,1,0:T(8,128)(2,1)} %get-tuple-element.41), channel_id=1, source_target_pairs={{0,1},{1,0},{2,3},{3,2},{4,5},{5,4},{6,7},{7,6},{8,9},{9,8},{10,11... | collective-permute-start | bytes 835592 | tf_op jit(solution)/shard_map/ppermute | solution.py:402
  44.1 9.8 %collective-permute-start.13 = (bf16[112,1024]{1,0:T(8,128)(2,1)}, bf16[112,1024]{1,0:T(8,128)(2,1)S(1)}, u32[]{:S(2)}, u32[]{:S(2)}) collective-permute-start(bf16[112,1024]{1,0:T(8,128)(2,1)} %get-tuple-element.44.refs_0_), channel_id=1, source_target_pairs={{0,1},{1,0},{2,3},{3,2},{4,5},{5,4},{6,7},{7,6},{8,9},{9,8},{10,11... | collective-permute-start | bytes 688136 | tf_op jit(solution)/shard_map/ppermute | solution.py:402
  49.9 8.2 %collective-permute-start.4 = (bf16[112,1024]{1,0:T(8,128)(2,1)S(1)}, bf16[112,1024]{1,0:T(8,128)(2,1)}, u32[]{:S(2)}, u32[]{:S(2)}) collective-permute-start(bf16[112,1024]{1,0:T(8,128)(2,1)S(1)} %collective-permute-done.3.refs_2_), channel_id=1, source_target_pairs={{0,2},{1,3},{2,4},{3,5},{4,6},{5,7},{6,8},{7,9},{8,10},{9,11},{10,... | collective-permute-start | bytes 688136 | tf_op jit(solution)/shard_map/ppermute | solution.py:399
  54.6 11.2 %collective-permute-start.9 = (bf16[3,112,512]{2,1,0:T(8,128)(2,1)S(1)}, bf16[3,112,512]{2,1,0:T(8,128)(2,1)S(1)}, u32[]{:S(2)}, u32[]{:S(2)}) collective-permute-start(bf16[3,112,512]{2,1,0:T(8,128)(2,1)S(1)} %collective-permute-done.8.refs_17_), channel_id=1, source_target_pairs={{0,14},{1,15},{2,0},{3,1},{4,2},{5,3},{6,4},{7,5},{8,6},{9,7},{10,... | collective-permute-start | bytes 1032200 | tf_op jit(solution)/shard_map/ppermute | solution.py:399
  58.1 11.8 %collective-permute-start.27 = (bf16[3,112,512]{2,1,0:T(8,128)(2,1)S(1)}, bf16[3,112,512]{2,1,0:T(8,128)(2,1)S(1)}, u32[]{:S(2)}, u32[]{:S(2)}) collective-permute-start(bf16[3,112,512]{2,1,0:T(8,128)(2,1)S(1)} %collective-permute-done.24.refs_16_), channel_id=1, source_target_pairs={{0,2},{1,3},{2,4},{3,5},{4,6},{5,7},{6,8},{7,9},{8,10},{9,11},{10,... | collective-permute-start | bytes 1032200 | tf_op jit(solution)/shard_map/ppermute | solution.py:399
  59.2 10.7 %collective-permute-start.25 = (bf16[3,112,512]{2,1,0:T(8,128)(2,1)S(1)}, bf16[3,112,512]{2,1,0:T(8,128)(2,1)S(1)}, u32[]{:S(2)}, u32[]{:S(2)}) collective-permute-start(bf16[3,112,512]{2,1,0:T(8,128)(2,1)S(1)} %collective-permute-done.24.refs_16_), channel_id=1, source_target_pairs={{0,1},{1,0},{2,3},{3,2},{4,5},{5,4},{6,7},{7,6},{8,9},{9,8},{10,11... | collective-permute-start | bytes 1032200 | tf_op jit(solution)/shard_map/ppermute | solution.py:402
  59.9 20.0 %collective-permute-start.26 = (bf16[3,112,512]{2,1,0:T(8,128)(2,1)S(1)}, bf16[3,112,512]{2,1,0:T(8,128)(2,1)S(1)}, u32[]{:S(2)}, u32[]{:S(2)}) collective-permute-start(bf16[3,112,512]{2,1,0:T(8,128)(2,1)S(1)} %collective-permute-done.8.refs_17_), channel_id=1, source_target_pairs={{0,1},{1,0},{2,3},{3,2},{4,5},{5,4},{6,7},{7,6},{8,9},{9,8},{10,11... | collective-permute-start | bytes 1032200 | tf_op jit(solution)/shard_map/ppermute | solution.py:402
  61.1 19.6 %collective-permute-start.5 = (bf16[112,1024]{1,0:T(8,128)(2,1)}, bf16[112,1024]{1,0:T(8,128)(2,1)}, u32[]{:S(2)}, u32[]{:S(2)}) collective-permute-start(bf16[112,1024]{1,0:T(8,128)(2,1)} %collective-permute-done.4.refs_6_), channel_id=1, source_target_pairs={{0,2},{1,3},{2,4},{3,5},{4,6},{5,7},{6,8},{7,9},{8,10},{9,11},{10,... | collective-permute-start | bytes 688136 | tf_op jit(solution)/shard_map/ppermute | solution.py:399
  65.8 15.4 %collective-permute-start.20 = (bf16[112,1024]{1,0:T(8,128)(2,1)}, bf16[112,1024]{1,0:T(8,128)(2,1)}, u32[]{:S(2)}, u32[]{:S(2)}) collective-permute-start(bf16[112,1024]{1,0:T(8,128)(2,1)} %collective-permute-done.17.refs_7_), channel_id=1, source_target_pairs={{0,14},{1,15},{2,0},{3,1},{4,2},{5,3},{6,4},{7,5},{8,6},{9,7},{10,... | collective-permute-start | bytes 688136 | tf_op jit(solution)/shard_map/ppermute | solution.py:399
  69.9 14.4 %collective-permute-start.10 = (bf16[3,112,512]{2,1,0:T(8,128)(2,1)S(1)}, bf16[3,112,512]{2,1,0:T(8,128)(2,1)}, u32[]{:S(2)}, u32[]{:S(2)}) collective-permute-start(bf16[3,112,512]{2,1,0:T(8,128)(2,1)S(1)} %collective-permute-done.9.refs_21_), channel_id=1, source_target_pairs={{0,14},{1,15},{2,0},{3,1},{4,2},{5,3},{6,4},{7,5},{8,6},{9,7},{10,... | collective-permute-start | bytes 1032200 | tf_op jit(solution)/shard_map/ppermute | solution.py:399
  70.6 15.7 %collective-permute-start.30 = (bf16[3,112,512]{2,1,0:T(8,128)(2,1)S(1)}, bf16[3,112,512]{2,1,0:T(8,128)(2,1)}, u32[]{:S(2)}, u32[]{:S(2)}) collective-permute-start(bf16[3,112,512]{2,1,0:T(8,128)(2,1)S(1)} %collective-permute-done.27.refs_20_), channel_id=1, source_target_pairs={{0,2},{1,3},{2,4},{3,5},{4,6},{5,7},{6,8},{7,9},{8,10},{9,11},{10,... | collective-permute-start | bytes 1032200 | tf_op jit(solution)/shard_map/ppermute | solution.py:399
  75.6 15.2 %all-to-all-start = ((bf16[8,8,2304]{2,1,0:T(8,128)(2,1)}), bf16[8,8,2304]{2,1,0:T(8,128)(2,1)S(1)}, u32[]{:S(2)}, u32[]{:S(2)}) async-start(bf16[8,8,2304]{2,1,0:T(8,128)(2,1)} %shard_map.75), calls=%async_computation | async-start | bytes 589824 | tf_op jit(solution)/shard_map/all_to_all | solution.py:438
  81.2 13.0 %collective-permute-start.28 = (bf16[3,112,512]{2,1,0:T(8,128)(2,1)S(1)}, bf16[3,112,512]{2,1,0:T(8,128)(2,1)}, u32[]{:S(2)}, u32[]{:S(2)}) collective-permute-start(bf16[3,112,512]{2,1,0:T(8,128)(2,1)S(1)} %collective-permute-done.27.refs_20_), channel_id=1, source_target_pairs={{0,1},{1,0},{2,3},{3,2},{4,5},{5,4},{6,7},{7,6},{8,9},{9,8},{10,11... | collective-permute-start | bytes 1032200 | tf_op jit(solution)/shard_map/ppermute | solution.py:402
  83.1 14.3 %collective-permute-start.29 = (bf16[3,112,512]{2,1,0:T(8,128)(2,1)S(1)}, bf16[3,112,512]{2,1,0:T(8,128)(2,1)}, u32[]{:S(2)}, u32[]{:S(2)}) collective-permute-start(bf16[3,112,512]{2,1,0:T(8,128)(2,1)S(1)} %collective-permute-done.9.refs_21_), channel_id=1, source_target_pairs={{0,1},{1,0},{2,3},{3,2},{4,5},{5,4},{6,7},{7,6},{8,9},{9,8},{10,11... | collective-permute-start | bytes 1032200 | tf_op jit(solution)/shard_map/ppermute | solution.py:402
  83.9 13.6 %collective-permute-start.21 = (bf16[112,1024]{1,0:T(8,128)(2,1)}, bf16[112,1024]{1,0:T(8,128)(2,1)}, u32[]{:S(2)}, u32[]{:S(2)}) collective-permute-start(bf16[112,1024]{1,0:T(8,128)(2,1)} %collective-permute-done.5.refs_10_), channel_id=1, source_target_pairs={{0,1},{1,0},{2,3},{3,2},{4,5},{5,4},{6,7},{7,6},{8,9},{9,8},{10,11... | collective-permute-start | bytes 688136 | tf_op jit(solution)/shard_map/ppermute | solution.py:402
  84.3 13.7 %collective-permute-start.6 = (bf16[112,1024]{1,0:T(8,128)(2,1)}, bf16[112,1024]{1,0:T(8,128)(2,1)}, u32[]{:S(2)}, u32[]{:S(2)}) collective-permute-start(bf16[112,1024]{1,0:T(8,128)(2,1)} %collective-permute-done.5.refs_10_), channel_id=1, source_target_pairs={{0,2},{1,3},{2,4},{3,5},{4,6},{5,7},{6,8},{7,9},{8,10},{9,11},{10,... | collective-permute-start | bytes 688136 | tf_op jit(solution)/shard_map/ppermute | solution.py:399
  86.3 13.7 %collective-permute-start.11 = (bf16[3,112,512]{2,1,0:T(8,128)(2,1)}, bf16[3,112,512]{2,1,0:T(8,128)(2,1)}, u32[]{:S(2)}, u32[]{:S(2)}) collective-permute-start(bf16[3,112,512]{2,1,0:T(8,128)(2,1)} %collective-permute-done.10.refs_25_), channel_id=1, source_target_pairs={{0,14},{1,15},{2,0},{3,1},{4,2},{5,3},{6,4},{7,5},{8,6},{9,7},{10,... | collective-permute-start | bytes 1032200 | tf_op jit(solution)/shard_map/ppermute | solution.py:399
  137.0 16.0 %collective-permute-start.41 = (bf16[2,8,1792]{2,1,0:T(8,128)(2,1)S(1)}, bf16[2,8,1792]{2,1,0:T(8,128)(2,1)S(1)}, u32[]{:S(2)}, u32[]{:S(2)}) collective-permute-start(bf16[2,8,1792]{2,1,0:T(8,128)(2,1)S(1)} %get-tuple-element.61), channel_id=1, source_target_pairs={{64,32},{192,160},{65,33},{193,161},{66,34},{194,162},{67,35},{195... | collective-permute-start | bytes 172040 | tf_op jit(solution)/shard_map/ppermute | solution.py:544
  138.3 14.7 %collective-permute-start.42 = (bf16[2,8,1792]{2,1,0:T(8,128)(2,1)S(1)}, bf16[2,8,1792]{2,1,0:T(8,128)(2,1)S(1)}, u32[]{:S(2)}, u32[]{:S(2)}) collective-permute-start(bf16[2,8,1792]{2,1,0:T(8,128)(2,1)S(1)} %get-tuple-element.61), channel_id=1, source_target_pairs={{64,96},{192,224},{65,97},{193,225},{66,98},{194,226},{67,99},{195... | collective-permute-start | bytes 172040 | tf_op jit(solution)/shard_map/ppermute | solution.py:545
  (54 other events, 428.7 us)
